TPU v7x, 32 devices: a whole 2x2x4 slice. The times are simulated.
32 devices in a mesh: dp: 8 (over y, x, core), mp: 4 (over z).
Axes of the slice: x: 2, y: 2, z: 4, core: 2. Of those that a mesh axis runs over, the one named last changes fastest.
Arguments:
- residues: bfloat16 [4096, 768], P('dp', 'mp'), may hold values from -6 to 6
- pair_input: bfloat16 [16, 256, 256, 256], P('dp', 'mp'), may hold values from -6 to 6
- out_grad: bfloat16 [4096, 768], P('dp', 'mp'), may hold values from -6 to 6
- bucket_layout: int32 [16], P('dp'), may hold values from 0 to 4
- time_bins: int32 [16, 4], P('dp'), may hold values from 0 to 63
- fold_class: int32 [16, 4], P('dp'), may hold values from 0 to 42
- attend_weight: float32 [768, 3, 768], P('dp', None, 'mp'), may hold values from -0.21875 to 0.21875
- attend_state: float32 [3, 768, 3, 768], P(None, 'dp', None, 'mp'), as said below
- merge_weight: float32 [768, 768], P('mp', 'dp'), may hold values from -0.625 to 0.625
- merge_state: float32 [3, 768, 768], P(None, 'mp', 'dp'), as said below
- expand_weight: float32 [768, 2, 3072], P('dp', None, 'mp'), may hold values from -0.21875 to 0.21875
- expand_state: float32 [3, 768, 2, 3072], P(None, 'dp', None, 'mp'), as said below
- shrink_weight: float32 [3072, 768], P('mp', 'dp'), may hold values from -0.109375 to 0.109375
- shrink_state: float32 [3, 3072, 768], P(None, 'mp', 'dp'), as said below
- modulate_weight: float32 [256, 6, 768], P('dp', None, 'mp'), may hold values from -0.375 to 0.375
- modulate_state: float32 [3, 256, 6, 768], P(None, 'dp', None, 'mp'), as said below
- pair_weight: float32 [256, 12], P('dp'), may hold values from -0.375 to 0.375
- pair_state: float32 [3, 256, 12], P(None, 'dp'), as said below
- class_weight: float32 [43, 256], P(None, 'dp'), may hold values from -4 to 4
- class_state: float32 [3, 43, 256], P(None, None, 'dp'), as said below
Outputs:
- output: bfloat16 [4096, 768], P('dp', 'mp')
- residue_grad: bfloat16 [4096, 768], P('dp', 'mp')
- pair_grad: bfloat16 [16, 256, 256, 256], P('dp', 'mp')
- attend_master: float32 [2, 768, 3, 768], P(None, 'dp', None, 'mp')
- attend_tracked: float32 [2, 768, 3, 768], P(None, 'dp', None, 'mp')
- merge_master: float32 [2, 768, 768], P(None, 'mp', 'dp')
- merge_tracked: float32 [2, 768, 768], P(None, 'mp', 'dp')
- expand_master: float32 [2, 768, 2, 3072], P(None, 'dp', None, 'mp')
- expand_tracked: float32 [2, 768, 2, 3072], P(None, 'dp', None, 'mp')
- shrink_master: float32 [2, 3072, 768], P(None, 'mp', 'dp')
- shrink_tracked: float32 [2, 3072, 768], P(None, 'mp', 'dp')
- modulate_master: float32 [2, 256, 6, 768], P(None, 'dp', None, 'mp')
- modulate_tracked: float32 [2, 256, 6, 768], P(None, 'dp', None, 'mp')
- pair_master: float32 [2, 256, 12], P(None, 'dp')
- pair_tracked: float32 [2, 256, 12], P(None, 'dp')
- class_master: float32 [2, 43, 256], P(None, None, 'dp')
- class_tracked: float32 [2, 43, 256], P(None, None, 'dp')
Inputs may be any that keep to these rules, and one draw needn't show every extreme that they name: `bucket_layout`: each window of 256 residues holds whole proteins: 0 one of 256, 1 two of 128, 2 one of 128 then two of 64, 3 two of 64 then one of 128, 4 four of 64. `time_bins`: slot s of a window describes its s-th protein; slots past the window's proteins are unused. `fold_class`: slot s of a window describes its s-th protein; slots past the window's proteins are unused. `attend_state`: slices hold the first moment, the second moment (positive) and the weights' average. `merge_state`: slices hold the first moment, the second moment (positive) and the weights' average. `expand_state`: slices hold the first moment, the second moment (positive) and the weights' average. `shrink_state`: slices hold the first moment, the second moment (positive) and the weights' average. `modulate_state`: slices hold the first moment, the second moment (positive) and the weights' average. `pair_state`: slices hold the first moment, the second moment (positive) and the weights' average. `class_state`: slices hold the first moment, the second moment (positive) and the weights' average.
All inputs are finite; a program needn't handle non-finite values.
Results may differ from a plain program's by a relative error of at most 0.015.
The roundings to bfloat16 on the way count: a program that leaves them out, or rounds other values in their place, can miss the bound.
Values may be sent and summed in bfloat16 or wider, within the bound.
A program may use at most 128 MiB of HBM per device.

v0:
```python
import math

import jax
import jax.numpy as jnp
import numpy as np
from jax import lax
from jax.sharding import PartitionSpec as P

D = 768
HD = 64
FF = 3072
PAIR = 256
CDIM = 256
TBINS = 64
STEP = 10


PATTERNS = np.array(
    [[0, 0, 0, 0], [0, 0, 1, 1], [0, 0, 1, 2], [0, 1, 2, 2], [0, 1, 2, 3]], dtype=np.int32
)
NORM_EPS = 1e-06
BETA_ONE = 0.9
BETA_TWO = 0.999
ADAM_EPS = 1e-08
DECAY = 0.01
AVERAGE = 0.999
MASKED = -1e30
HIGH = lax.Precision.HIGHEST


def time_features(bins, width):
    half = width // 2
    moment = (bins.astype(jnp.float32) + 0.5) / TBINS
    freq = jnp.exp(-math.log(10000.0) * jnp.arange(half, dtype=jnp.float32) / half)
    angle = 1000.0 * moment[..., None] * freq
    return jnp.concatenate([jnp.sin(angle), jnp.cos(angle)], axis=-1)


def slot_ids(layout, window):
    unit = np.arange(window) // (window // 4)
    table = jnp.asarray(PATTERNS[:, unit])
    select = (layout[:, None] == jnp.arange(5, dtype=jnp.int32)[None, :]).astype(jnp.int32)
    return jnp.dot(select, table)


def adamw(master, state, grad, rate):
    first = BETA_ONE * state[0] + (1.0 - BETA_ONE) * grad
    second = BETA_TWO * state[1] + (1.0 - BETA_TWO) * grad * grad
    first_hat = first / (1.0 - BETA_ONE**STEP)
    second_hat = second / (1.0 - BETA_TWO**STEP)
    updated = master - rate * (first_hat / (jnp.sqrt(second_hat) + ADAM_EPS) + DECAY * master)
    average = AVERAGE * state[2] + (1.0 - AVERAGE) * updated
    return (jnp.stack([updated, average]), jnp.stack([first, second]))


def normalize(hidden, shift, scale, width):
    totals = lax.psum((jnp.sum(hidden, axis=1), jnp.sum(hidden * hidden, axis=1)), "mp")
    center = totals[0] / width
    spread = lax.rsqrt(totals[1] / width - center * center + NORM_EPS)
    normed = (hidden - center[:, None]) * spread[:, None]
    rows = (normed * (1.0 + scale) + shift).astype(jnp.bfloat16)
    return (normed, spread, lax.all_gather(rows, "mp", axis=1, tiled=True))


def normalize_back(partial_value, normed, spread, scale, width):
    upstream = lax.psum_scatter(partial_value, "mp", scatter_dimension=1, tiled=True)
    inner = upstream * (1.0 + scale)
    totals = lax.psum((jnp.sum(inner, axis=1), jnp.sum(inner * normed, axis=1)), "mp")
    result = spread[:, None] * (
        inner - totals[0][:, None] / width - normed * (totals[1][:, None] / width)
    )
    return (upstream, result)


def branch_total(partial_value):
    return lax.psum_scatter(partial_value, "mp", scatter_dimension=1, tiled=True)


def gather_grad(value):
    return lax.all_gather(value, "mp", axis=1, tiled=True)


def attention_scores(query, keys, bias, same, factor):
    scores = jnp.einsum(
        "wihe,wjhe->whij", query, keys, preferred_element_type=jnp.float32
    ) * factor + bias.astype(jnp.float32)
    return jnp.where(same[:, None], scores, MASKED)


def local(
    residues,
    pair_input,
    out_grad,
    bucket_layout,
    time_bins,
    fold_class,
    attend_weight,
    attend_state,
    merge_weight,
    merge_state,
    expand_weight,
    expand_state,
    shrink_weight,
    shrink_state,
    modulate_weight,
    modulate_state,
    pair_weight,
    pair_state,
    class_weight,
    class_state,
):
    parts = lax.axis_size("mp")
    gathered = (
        lax.all_gather(attend_weight.astype(jnp.bfloat16), "dp", axis=0, tiled=True),
        lax.all_gather(merge_weight.astype(jnp.bfloat16), "dp", axis=1, tiled=True),
        lax.all_gather(expand_weight.astype(jnp.bfloat16), "dp", axis=0, tiled=True),
        lax.all_gather(shrink_weight.astype(jnp.bfloat16), "dp", axis=1, tiled=True),
        lax.all_gather(modulate_weight.astype(jnp.bfloat16), "dp", axis=0, tiled=True),
        lax.all_gather(pair_weight.astype(jnp.bfloat16), "dp", axis=0, tiled=True),
        lax.all_gather(class_weight.astype(jnp.bfloat16), "dp", axis=1, tiled=True),
    )
    attend_full, merge_full, expand_full, shrink_full, modulate_full, pair_full, class_full = (
        gathered
    )
    tokens, local_width = residues.shape
    windows = bucket_layout.shape[0]
    window = tokens // windows
    slots = time_bins.shape[1]
    classes_count = class_full.shape[0]
    heads_local = local_width // HD
    width = local_width * parts
    factor = HD ** (-0.5)
    slot = slot_ids(bucket_layout, window)
    pick = (slot[..., None] == jnp.arange(slots, dtype=jnp.int32)).astype(jnp.float32)
    same = slot[:, :, None] == slot[:, None, :]
    class_pick = (fold_class[..., None] == jnp.arange(classes_count, dtype=jnp.int32)).astype(
        jnp.float32
    )
    before = time_features(time_bins, class_full.shape[1]) + jnp.einsum(
        "wsn,nc->wsc", class_pick, class_full.astype(jnp.float32), precision=HIGH
    )
    condition = jax.nn.silu(before).astype(jnp.bfloat16)
    modulation = jnp.einsum(
        "wsc,cjd->wsjd", condition, modulate_full, preferred_element_type=jnp.float32
    )
    per_token = jnp.einsum("wts,wsjd->wtjd", pick, modulation, precision=HIGH).reshape(
        tokens, 6, local_width
    )
    hidden_in = residues.astype(jnp.float32)
    normed_one, spread_one, rows_one = normalize(hidden_in, per_token[:, 0], per_token[:, 1], width)
    triple = jnp.einsum(
        "td,dje->tje", rows_one, attend_full, preferred_element_type=jnp.float32
    ).astype(jnp.bfloat16)
    query = triple[:, 0].reshape(windows, window, heads_local, HD)
    keys = triple[:, 1].reshape(windows, window, heads_local, HD)
    values = triple[:, 2].reshape(windows, window, heads_local, HD)
    local_bias = jnp.einsum(
        "wijc,ch->whij", pair_input, pair_full, preferred_element_type=jnp.float32
    ).astype(jnp.bfloat16)
    bias = lax.all_to_all(local_bias, "mp", split_axis=1, concat_axis=2, tiled=True)
    scores = attention_scores(query, keys, bias, same, factor)
    peak = jnp.max(scores, axis=-1, keepdims=True)
    logsum = peak + jnp.log(jnp.sum(jnp.exp(scores - peak), axis=-1, keepdims=True))
    chance = jnp.exp(scores - logsum).astype(jnp.bfloat16)
    mixed = (
        jnp.einsum("whij,wjhe->wihe", chance, values, preferred_element_type=jnp.float32)
        .astype(jnp.bfloat16)
        .reshape(tokens, local_width)
    )
    attended = branch_total(jnp.dot(mixed, merge_full, preferred_element_type=jnp.float32))
    middle = hidden_in + per_token[:, 2] * attended
    normed_two, spread_two, rows_two = normalize(middle, per_token[:, 3], per_token[:, 4], width)
    pair_up = jnp.einsum("td,dje->tje", rows_two, expand_full, preferred_element_type=jnp.float32)
    gate = pair_up[:, 0]
    upward = pair_up[:, 1]
    sigma = jax.nn.sigmoid(gate)
    activated = (gate * sigma * upward).astype(jnp.bfloat16)
    fed = branch_total(jnp.dot(activated, shrink_full, preferred_element_type=jnp.float32))
    output = (middle + per_token[:, 5] * fed).astype(jnp.bfloat16)
    upper = out_grad.astype(jnp.float32)
    fed_grad = gather_grad((per_token[:, 5] * upper).astype(jnp.bfloat16))
    act_grad = lax.dot_general(
        fed_grad, shrink_full, (((1,), (1,)), ((), ())), preferred_element_type=jnp.float32
    )
    shrink_grad = lax.dot_general(
        activated, fed_grad, (((0,), (0,)), ((), ())), preferred_element_type=jnp.float32
    )
    slope = sigma * (1.0 + gate * (1.0 - sigma))
    up_grads = jnp.stack([act_grad * upward * slope, act_grad * gate * sigma], axis=1).astype(
        jnp.bfloat16
    )
    expand_grad = jnp.einsum("td,tje->dje", rows_two, up_grads, preferred_element_type=jnp.float32)
    partial_two = jnp.einsum(
        "tje,dje->td", up_grads, expand_full, preferred_element_type=jnp.float32
    )
    upstream_two, norm_two = normalize_back(
        partial_two, normed_two, spread_two, per_token[:, 4], width
    )
    middle_grad = upper + norm_two
    merged_grad = gather_grad((per_token[:, 2] * middle_grad).astype(jnp.bfloat16))
    mixed_grad = (
        lax.dot_general(
            merged_grad, merge_full, (((1,), (1,)), ((), ())), preferred_element_type=jnp.float32
        )
        .astype(jnp.bfloat16)
        .reshape(windows, window, heads_local, HD)
    )
    merge_grad = lax.dot_general(
        mixed, merged_grad, (((0,), (0,)), ((), ())), preferred_element_type=jnp.float32
    )
    again = attention_scores(query, keys, bias, same, factor)
    exact = jnp.exp(again - logsum)
    chance_grad = jnp.einsum(
        "wihe,wjhe->whij", mixed_grad, values, preferred_element_type=jnp.float32
    )
    score_grad = (
        exact * (chance_grad - jnp.sum(exact * chance_grad, axis=-1, keepdims=True))
    ).astype(jnp.bfloat16)
    value_grad = jnp.einsum(
        "whij,wihe->wjhe",
        exact.astype(jnp.bfloat16),
        mixed_grad,
        preferred_element_type=jnp.float32,
    )
    query_grad = (
        jnp.einsum("whij,wjhe->wihe", score_grad, keys, preferred_element_type=jnp.float32) * factor
    )
    keys_grad = (
        jnp.einsum("whij,wihe->wjhe", score_grad, query, preferred_element_type=jnp.float32)
        * factor
    )
    triple_grad = jnp.stack(
        [
            query_grad.reshape(tokens, local_width),
            keys_grad.reshape(tokens, local_width),
            value_grad.reshape(tokens, local_width),
        ],
        axis=1,
    ).astype(jnp.bfloat16)
    bias_grad = lax.all_to_all(score_grad, "mp", split_axis=2, concat_axis=1, tiled=True)
    pair_grad = jnp.einsum(
        "whij,ch->wijc", bias_grad, pair_full, preferred_element_type=jnp.float32
    ).astype(jnp.bfloat16)
    pairwise_grad = jnp.einsum(
        "wijc,whij->ch", pair_input, bias_grad, preferred_element_type=jnp.float32
    )
    attend_grad = jnp.einsum(
        "td,tje->dje", rows_one, triple_grad, preferred_element_type=jnp.float32
    )
    partial_one = jnp.einsum(
        "tje,dje->td", triple_grad, attend_full, preferred_element_type=jnp.float32
    )
    upstream_one, norm_one = normalize_back(
        partial_one, normed_one, spread_one, per_token[:, 1], width
    )
    residue_grad = (middle_grad + norm_one).astype(jnp.bfloat16)
    token_mod_grad = jnp.stack(
        [
            upstream_one,
            upstream_one * normed_one,
            middle_grad * attended,
            upstream_two,
            upstream_two * normed_two,
            upper * fed,
        ],
        axis=1,
    ).reshape(windows, window, 6, local_width)
    mod_grad = jnp.einsum("wts,wtjd->wsjd", pick, token_mod_grad, precision=HIGH)
    modulate_grad = jnp.einsum(
        "wsc,wsjd->cjd", condition.astype(jnp.float32), mod_grad, precision=HIGH
    )
    cond_grad = jnp.einsum(
        "wsjd,cjd->wsc", mod_grad, modulate_full.astype(jnp.float32), precision=HIGH
    )
    sig_before = jax.nn.sigmoid(before)
    before_grad = cond_grad * (sig_before * (1.0 + before * (1.0 - sig_before)))
    class_grad = jnp.einsum("wsn,wsc->nc", class_pick, before_grad, precision=HIGH)
    shared = lax.psum((pairwise_grad, class_grad), "mp")
    sums = (
        lax.psum_scatter(attend_grad, "dp", scatter_dimension=0, tiled=True),
        lax.psum_scatter(merge_grad, "dp", scatter_dimension=1, tiled=True),
        lax.psum_scatter(expand_grad, "dp", scatter_dimension=0, tiled=True),
        lax.psum_scatter(shrink_grad, "dp", scatter_dimension=1, tiled=True),
        lax.psum_scatter(modulate_grad, "dp", scatter_dimension=0, tiled=True),
        lax.psum_scatter(shared[0], "dp", scatter_dimension=0, tiled=True),
        lax.psum_scatter(shared[1], "dp", scatter_dimension=1, tiled=True),
    )
    rates = (
        2.0 / math.sqrt(D),
        2.0 / math.sqrt(D // 8),
        2.0 / math.sqrt(D),
        2.0 / math.sqrt(FF),
        2.0 / math.sqrt(CDIM),
        2.0 / math.sqrt(PAIR),
        2.0,
    )
    masters = (
        attend_weight,
        merge_weight,
        expand_weight,
        shrink_weight,
        modulate_weight,
        pair_weight,
        class_weight,
    )
    states = (
        attend_state,
        merge_state,
        expand_state,
        shrink_state,
        modulate_state,
        pair_state,
        class_state,
    )
    results = []
    for index in range(7):
        updated, tracked = adamw(masters[index], states[index], sums[index], rates[index])
        results.append(updated)
        results.append(tracked)
    return (
        output,
        residue_grad,
        pair_grad,
        results[0],
        results[1],
        results[2],
        results[3],
        results[4],
        results[5],
        results[6],
        results[7],
        results[8],
        results[9],
        results[10],
        results[11],
        results[12],
        results[13],
    )


def solution(mesh):
    placed = (
        P("dp", "mp"),
        P("dp", "mp", None, None),
        P("dp", "mp"),
        P("dp"),
        P("dp", None),
        P("dp", None),
        P("dp", None, "mp"),
        P(None, "dp", None, "mp"),
        P("mp", "dp"),
        P(None, "mp", "dp"),
        P("dp", None, "mp"),
        P(None, "dp", None, "mp"),
        P("mp", "dp"),
        P(None, "mp", "dp"),
        P("dp", None, "mp"),
        P(None, "dp", None, "mp"),
        P("dp", None),
        P(None, "dp", None),
        P(None, "dp"),
        P(None, None, "dp"),
    )
    return jax.shard_map(
        local,
        mesh=mesh,
        in_specs=placed,
        out_specs=(
            P("dp", "mp"),
            P("dp", "mp"),
            P("dp", "mp", None, None),
            P(None, "dp", None, "mp"),
            P(None, "dp", None, "mp"),
            P(None, "mp", "dp"),
            P(None, "mp", "dp"),
            P(None, "dp", None, "mp"),
            P(None, "dp", None, "mp"),
            P(None, "mp", "dp"),
            P(None, "mp", "dp"),
            P(None, "dp", None, "mp"),
            P(None, "dp", None, "mp"),
            P(None, "dp", None),
            P(None, "dp", None),
            P(None, None, "dp"),
            P(None, None, "dp"),
        ),
        check_vma=False,
    )
```

profile of v0, /device:TPU:0, one launch (start us, length us, event | category | flops | bytes accessed | tf_op | source)
XLA Modules:
  0.0 695.3 jit_solution(10774368603237284982)
XLA Ops:
  8.7 10.6 %all-gather = bf16[8,32,12]{1,2,0:T(8,128)(2,1)S(1)} all-gather(bf16[1,32,12]{1,2,0:T(8,128)(2,1)S(1)} %convert_bitcast_fusion.1), channel_id=1, replica_groups=mesh['dp'=8,'mp'=4] {'dp'}, dimensions={0}, use_global_device_ids=true | all-gather | bytes 6912 | tf_op jit(solution)/shard_map/all_gather | solution.py:119
  19.4 10.2 %fusion.2 = bf16[2,12,64,256]{3,1,2,0:T(8,128)(2,1)S(1)} fusion(bf16[2,64,256,256]{3,2,1,0:T(8,128)(2,1)} %param.22, bf16[256,12,1,1]{0,1,2,3:T(8,128)(2,1)S(1)} %reshape.153), kind=kOutput, calls=%fused_computation.21 | convolution fusion | flops 201719808 | bytes 17569792 | tf_op jit(solution)/shard_map/wijc,ch->whij/dot_general | solution.py:157
  30.8 5.0 all-to-all-start
  36.5 9.2 %all_gather.33 = bf16[43,256]{0,1:T(8,128)(2,1)S(1)} all-gather(bf16[43,32]{0,1:T(8,128)(2,1)S(1)} %convert_element_type.105), channel_id=1, replica_groups=mesh['dp'=8,'mp'=4] {'dp'}, dimensions={1}, use_global_device_ids=true | all-gather | bytes 24768 | tf_op jit(solution)/shard_map/all_gather | solution.py:120
  45.9 9.4 %all_gather.34 = bf16[256,6,192]{2,0,1:T(8,128)(2,1)S(1)} all-gather(bf16[32,6,192]{2,0,1:T(8,128)(2,1)S(1)} %convert_element_type.107), channel_id=1, replica_groups=mesh['dp'=8,'mp'=4] {'dp'}, dimensions={0}, use_global_device_ids=true | all-gather | bytes 663552 | tf_op jit(solution)/shard_map/all_gather | solution.py:118
  57.6 12.9 %all-reduce.3 = (f32[512]{0:T(512)}, f32[512]{0:T(512)}) all-reduce(f32[512]{0:T(512)} %get-tuple-element.109, f32[512]{0:T(512)} %get-tuple-element.108), channel_id=1, replica_groups=mesh['dp'=8,'mp'=4] {'mp'}, use_global_device_ids=true, to_apply=%region_3.4 | all-reduce | flops 1024 | bytes 8192 | tf_op jit(solution)/shard_map/psum | solution.py:57
  72.0 13.0 %all_gather.36 = bf16[768,3,192]{2,1,0:T(4,128)(2,1)} all-gather(bf16[96,3,192]{2,1,0:T(4,128)(2,1)S(1)} %copy.218), channel_id=1, replica_groups=mesh['dp'=8,'mp'=4] {'dp'}, dimensions={0}, use_global_device_ids=true | all-gather | bytes 995328 | tf_op jit(solution)/shard_map/all_gather | solution.py:114
  86.6 3.4 copy.219
  90.0 17.8 %all_gather.35 = bf16[512,768]{0,1:T(8,128)(2,1)S(1)} all-gather(bf16[512,192]{0,1:T(8,128)(2,1)S(1)} %copy-done.37), channel_id=1, replica_groups=mesh['dp'=8,'mp'=4] {'mp'}, dimensions={1}, use_global_device_ids=true | all-gather | bytes 983040 | tf_op jit(solution)/shard_map/all_gather | solution.py:62
  107.8 2.1 fusion.122
  110.8 9.6 %all_gather.38 = bf16[192,768]{0,1:T(8,128)(2,1)S(1)} all-gather(bf16[192,96]{0,1:T(8,128)(2,1)S(1)} %copy-done.41), channel_id=1, replica_groups=mesh['dp'=8,'mp'=4] {'dp'}, dimensions={1}, use_global_device_ids=true | all-gather | bytes 331776 | tf_op jit(solution)/shard_map/all_gather | solution.py:115
  124.4 1.9 fusion.120
  132.9 30.7 %reduce-scatter.16.cloned.1.call-done = f32[512,192]{0,1:T(8,128)} async-done(((f32[512,768]{0,1:T(8,128)}), f32[512,192]{0,1:T(8,128)}) %reduce-scatter.16.cloned.1.call-update) | async-done | bytes 393232 | tf_op jit(solution)/shard_map/reduce_scatter | solution.py:76
  164.8 9.8 %all-reduce.2 = (f32[512]{0:T(512)S(1)}, f32[512]{0:T(512)S(1)}) all-reduce(f32[512]{0:T(512)S(1)} %get-tuple-element.107, f32[512]{0:T(512)S(1)} %get-tuple-element.106), channel_id=1, replica_groups=mesh['dp'=8,'mp'=4] {'mp'}, use_global_device_ids=true, to_apply=%region_10.11 | all-reduce | flops 1024 | bytes 8192 | tf_op jit(solution)/shard_map/psum | solution.py:57
  176.1 17.5 %all_gather.42 = bf16[512,768]{0,1:T(8,128)(2,1)} all-gather(bf16[512,192]{0,1:T(8,128)(2,1)S(1)} %get-tuple-element.141), channel_id=1, replica_groups=mesh['dp'=8,'mp'=4] {'mp'}, dimensions={1}, use_global_device_ids=true | all-gather | bytes 983040 | tf_op jit(solution)/shard_map/all_gather | solution.py:80
  193.7 16.7 %all_gather.39 = bf16[512,768]{0,1:T(8,128)(2,1)} all-gather(bf16[512,192]{0,1:T(8,128)(2,1)S(1)} %get-tuple-element.142), channel_id=1, replica_groups=mesh['dp'=8,'mp'=4] {'mp'}, dimensions={1}, use_global_device_ids=true | all-gather | bytes 983040 | tf_op jit(solution)/shard_map/all_gather | solution.py:62
  210.4 5.0 fusion.20
  215.4 4.8 fusion.26
  221.3 2.6 convolution_bitcast_fusion.2
  224.0 3.5 fusion.121
  227.5 32.7 %reduce-scatter.20.cloned.1.call-done = f32[512,192]{0,1:T(8,128)} async-done(((f32[512,768]{0,1:T(8,128)}), f32[512,192]{0,1:T(8,128)}) %reduce-scatter.20.cloned.1.call-update) | async-done | bytes 393232 | tf_op jit(solution)/shard_map/reduce_scatter | solution.py:66
  261.5 9.7 %all-reduce.1 = (f32[512]{0:T(512)S(1)}, f32[512]{0:T(512)S(1)}) all-reduce(f32[512]{0:T(512)S(1)} %get-tuple-element.105, f32[512]{0:T(512)S(1)} %get-tuple-element.104), channel_id=1, replica_groups=mesh['dp'=8,'mp'=4] {'mp'}, use_global_device_ids=true, to_apply=%region_16.17 | all-reduce | flops 1024 | bytes 8192 | tf_op jit(solution)/shard_map/psum | solution.py:68
  271.8 25.1 %reduce-scatter.18.cloned.1.call-done = f32[512,192]{0,1:T(8,128)} async-done(((f32[512,768]{0,1:T(8,128)}), f32[512,192]{0,1:T(8,128)}) %reduce-scatter.18.cloned.1.call-update) | async-done | bytes 393232 | tf_op jit(solution)/shard_map/reduce_scatter | solution.py:76
  296.9 2.8 fusion.117
  301.5 17.9 %all_gather.43 = bf16[512,768]{0,1:T(8,128)(2,1)S(1)} all-gather(bf16[512,192]{0,1:T(8,128)(2,1)S(1)} %multiply_convert_fusion.4), channel_id=1, replica_groups=mesh['dp'=8,'mp'=4] {'mp'}, dimensions={1}, use_global_device_ids=true | all-gather | bytes 983040 | tf_op jit(solution)/shard_map/all_gather | solution.py:80
  329.9 2.0 convolution_bitcast_fusion.1
  333.3 2.2 fusion.124
  337.3 3.5 all-to-all-start.1
  342.2 37.7 %all-to-all-done.1 = bf16[2,3,256,256]{3,0,1,2:T(2,128)(2,1)S(1)} async-done(((bf16[2,3,256,256]{3,0,1,2:T(2,128)(2,1)}), bf16[2,3,256,256]{3,0,1,2:T(2,128)(2,1)S(1)}, u32[]{:S(2)}, u32[]{:S(2)}) %all-to-all-start.1) | async-done | bytes 786464 | tf_op jit(solution)/shard_map/all_to_all | solution.py:240
  380.1 7.4 %fusion.10 = f32[256,12]{0,1:T(8,128)S(1)} fusion(bf16[2,64,256,256]{3,2,1,0:T(8,128)(2,1)} %param.22, bf16[2,12,64,256]{3,2,1,0:T(8,128)(2,1)S(1)} %bitcast.411), kind=kOutput, calls=%fused_computation.38 | convolution fusion | flops 201326592 | bytes 17575936 | tf_op jit(solution)/shard_map/wijc,whij->ch/dot_general | solution.py:244
  388.6 2.3 fusion.17
  394.4 2.1 fusion.115
  396.5 2.1 stack.192
  405.4 5.2 fusion.16
  410.6 3.1 fusion.118
  413.7 14.0 %reduce-scatter.28.cloned.1.call-done = f32[768,96]{0,1:T(8,128)} async-done(((f32[768,768]{0,1:T(8,128)}), f32[768,96]{0,1:T(8,128)}) %reduce-scatter.28.cloned.1.call-update) | async-done | bytes 294928 | tf_op jit(solution)/shard_map/reduce_scatter | solution.py:283
  430.5 35.8 %reduce-scatter.34.cloned.1.call-done = f32[96,192]{1,0:T(8,128)} async-done(((f32[768,192]{1,0:T(8,128)}), f32[96,192]{1,0:T(8,128)}) %reduce-scatter.34.cloned.1.call-update) | async-done | bytes 73744
  469.7 8.6 %convolution_convert_fusion = bf16[2,64,256,256]{3,2,1,0:T(8,128)(2,1)} fusion(bf16[2,12,64,256]{3,2,1,0:T(8,128)(2,1)S(1)} %bitcast.412, bf16[256,12,1,1]{0,1,2,3:T(8,128)(2,1)S(1)} %reshape.153), kind=kOutput, calls=%fused_computation.2 | convolution fusion | flops 209715200 | bytes 17569792 | tf_op jit(solution)/shard_map/whij,ch->wijc/dot_general | solution.py:241
  478.3 25.2 %reduce-scatter.36.cloned.1.call-done = f32[32,12]{1,0:T(8,128)} async-done(((f32[256,12]{1,0:T(8,128)}), f32[32,12]{1,0:T(8,128)}) %reduce-scatter.36.cloned.1.call-update) | async-done | bytes 1552
  504.2 44.9 %reduce-scatter.24.cloned.1.call-done = f32[96,3,192]{2,0,1:T(8,128)} async-done(((f32[768,3,192]{2,0,1:T(8,128)}), f32[96,3,192]{2,0,1:T(8,128)}) %reduce-scatter.24.cloned.1.call-update) | async-done | bytes 221200 | tf_op jit(solution)/shard_map/reduce_scatter | solution.py:280
  552.4 2.1 convolution_bitcast_fusion.3
  554.6 31.8 %reduce-scatter.32.cloned.1.call-done = f32[43,32]{0,1:T(8,128)} async-done(((f32[43,256]{0,1:T(8,128)}), f32[43,32]{0,1:T(8,128)}) %reduce-scatter.32.cloned.1.call-update) | async-done | bytes 5520 | tf_op jit(solution)/shard_map/reduce_scatter | solution.py:286
  586.4 19.3 %all-reduce = (f32[512]{0:T(512)S(1)}, f32[512]{0:T(512)S(1)}, f32[32,12]{0,1:T(8,128)S(1)}, f32[43,32]{0,1:T(8,128)S(1)}) all-reduce(f32[512]{0:T(512)S(1)} %get-tuple-element.103, f32[512]{0:T(512)S(1)} %get-tuple-element.102, f32[32,12]{0,1:T(8,128)S(1)} %copy.279, ...), channel_id=1, replica_groups=mesh['dp'=8,'mp'=4] {'mp'}, use_global_device_ids=true, to_apply=%region_22.23 | all-reduce | flops 2784 | bytes 22272 | tf_op jit(solution)/shard_map/psum | solution.py:68
  608.2 1.8 fusion.46
  610.1 33.4 %reduce-scatter.26.cloned.1.call-done = f32[96,2,768]{2,0,1:T(8,128)} async-done(((f32[768,2,768]{2,0,1:T(8,128)}), f32[96,2,768]{2,0,1:T(8,128)}) %reduce-scatter.26.cloned.1.call-update) | async-done | bytes 589840 | tf_op jit(solution)/shard_map/reduce_scatter | solution.py:282
  645.3 1.9 copy.262
  647.3 1.9 copy.263
  649.2 35.9 %reduce-scatter.30.cloned.1.call-done = f32[32,6,192]{2,0,1:T(8,128)} async-done(((f32[256,6,192]{2,0,1:T(8,128)}), f32[32,6,192]{2,0,1:T(8,128)}) %reduce-scatter.30.cloned.1.call-update) | async-done | bytes 147472 | tf_op jit(solution)/shard_map/reduce_scatter | solution.py:284
  (270 shorter events, 70.7 us)
Async XLA Ops:
  29.6 6.2 copy-start.5
  29.6 6.9 copy-start.44
  29.7 16.1 %copy-start.34 = (f32[32,6,192]{2,0,1:T(8,128)S(1)}, f32[32,6,192]{2,0,1:T(8,128)}, u32[]{:S(2)}) copy-start(f32[32,6,192]{2,0,1:T(8,128)} %param.35) | copy-start | bytes 442372
  29.7 16.1 %copy-start.29 = (f32[96,3,192]{2,0,1:T(8,128)S(1)}, f32[96,3,192]{2,0,1:T(8,128)}, u32[]{:S(2)}) copy-start(f32[96,3,192]{2,0,1:T(8,128)} %param.27) | copy-start | bytes 663556
  30.8 24.5 %copy-start.64 = (s32[2]{0:T(128)S(1)}, s32[2]{0:T(128)}, u32[]{:S(2)}) copy-start(s32[2]{0:T(128)} %param.24) | copy-start | bytes 28
  30.8 24.5 %copy-start.65 = (s32[5,256]{1,0:T(8,128)S(1)}, s32[5,256]{1,0:T(8,128)}, u32[]{:S(2)}) copy-start(s32[5,256]{1,0:T(8,128)} %constant.50.clone) | copy-start | bytes 15364
  30.8 24.9 %copy-start.60 = (s32[2,4]{1,0:T(2,128)S(1)}, s32[2,4]{1,0:T(2,128)}, u32[]{:S(2)}) copy-start(s32[2,4]{1,0:T(2,128)} %param.26) | copy-start | bytes 100
  30.8 90.4 %all-to-all-start = ((bf16[2,12,64,256]{3,2,0,1:T(8,128)(2,1)}), bf16[2,12,64,256]{3,2,0,1:T(8,128)(2,1)}, u32[]{:S(2)}, u32[]{:S(2)}) async-start(bf16[2,12,64,256]{3,2,0,1:T(8,128)(2,1)} %copy.223), calls=%async_computation | async-start | bytes 1572864 | tf_op jit(solution)/shard_map/all_to_all | solution.py:160
  35.8 127.8 %reduce-scatter.16.cloned.1.call-start = ((), (), s32[]{:S(2)}) async-start(), calls=%async_computation.13 | async-start | bytes 1966080 | tf_op jit(solution)/shard_map/reduce_scatter | solution.py:76
  57.6 32.4 %copy-start = (f32[2,6,24,8,256]{4,3,0,2,1:T(8,128)}, f32[2,6,24,8,256]{4,3,0,2,1:T(8,128)S(1)}, u32[]{:S(2)}) copy-start(f32[2,6,24,8,256]{4,3,0,2,1:T(8,128)S(1)} %copy.283) | copy-start | bytes 7077892
  71.2 18.8 %copy-start.47 = (f32[512]{0:T(512)}, f32[512]{0:T(512)S(1)}, u32[]{:S(2)}) copy-start(f32[512]{0:T(512)S(1)} %get-tuple-element.180) | copy-start | bytes 6148
  71.2 18.8 %copy-start.49 = (f32[512]{0:T(512)}, f32[512]{0:T(512)S(1)}, u32[]{:S(2)}) copy-start(f32[512]{0:T(512)S(1)} %get-tuple-element.181) | copy-start | bytes 6148
  110.0 10.4 %copy-start.57 = (s32[2,256]{1,0:T(2,128)S(1)}, s32[2,256]{1,0:T(2,128)}, u32[]{:S(2)}) copy-start(s32[2,256]{1,0:T(2,128)} %copy-done.56) | copy-start | bytes 6148
  110.1 16.4 %copy-start.21 = (bf16[2,256,3,64]{1,0,3,2:T(2,128)(2,1)}, bf16[2,256,3,64]{1,0,3,2:T(2,128)(2,1)S(1)}, u32[]{:S(2)}) copy-start(bf16[2,256,3,64]{1,0,3,2:T(2,128)(2,1)S(1)} %reshape_squeeze.9) | copy-start | bytes 589828
  110.8 13.6 %copy-start.17 = (bf16[2,256,3,64]{1,0,3,2:T(2,128)(2,1)}, bf16[2,256,3,64]{1,0,3,2:T(2,128)(2,1)S(1)}, u32[]{:S(2)}) copy-start(bf16[2,256,3,64]{1,0,3,2:T(2,128)(2,1)S(1)} %reshape_squeeze.10) | copy-start | bytes 589828
  120.4 6.8 copy-start.11
  129.4 45.3 %copy-start.33 = (bf16[512,192]{0,1:T(8,128)(2,1)S(1)}, bf16[512,192]{0,1:T(8,128)(2,1)}, u32[]{:S(2)}) copy-start(bf16[512,192]{0,1:T(8,128)(2,1)} %param.23) | copy-start | bytes 589828
  129.4 81.0 %all-gather.4.cloned.1.call-start = ((), (), s32[]{:S(2)}) async-start(), calls=%async_computation.14 | async-start | bytes 2654208 | tf_op jit(solution)/shard_map/all_gather | solution.py:116
  131.2 84.2 %all-gather.6.cloned.1.call-start = ((), (), s32[]{:S(2)}) async-start(), calls=%async_computation.15 | async-start | bytes 1327104 | tf_op jit(solution)/shard_map/all_gather | solution.py:117
  132.9 127.4 %reduce-scatter.20.cloned.1.call-start = ((), (), s32[]{:S(2)}) async-start(), calls=%async_computation.17 | async-start | bytes 1966080 | tf_op jit(solution)/shard_map/reduce_scatter | solution.py:66
  174.7 19.0 %copy-start.52 = (f32[512]{0:T(512)}, f32[512]{0:T(512)S(1)}, u32[]{:S(2)}) copy-start(f32[512]{0:T(512)S(1)} %get-tuple-element.178) | copy-start | bytes 6148
  174.7 19.0 %copy-start.54 = (f32[512]{0:T(512)}, f32[512]{0:T(512)S(1)}, u32[]{:S(2)}) copy-start(f32[512]{0:T(512)S(1)} %get-tuple-element.179) | copy-start | bytes 6148
  223.9 73.0 %reduce-scatter.18.cloned.1.call-start = ((), (), s32[]{:S(2)}) async-start(), calls=%async_computation.16 | async-start | bytes 1966080 | tf_op jit(solution)/shard_map/reduce_scatter | solution.py:76
  227.4 32.8 %copy-start.53 = (f32[512]{0:T(512)S(1)}, f32[512]{0:T(512)}, u32[]{:S(2)}) copy-start(f32[512]{0:T(512)} %copy-done.52) | copy-start | bytes 6148
  227.5 32.8 %copy-start.55 = (f32[512]{0:T(512)S(1)}, f32[512]{0:T(512)}, u32[]{:S(2)}) copy-start(f32[512]{0:T(512)} %copy-done.54) | copy-start | bytes 6148
  227.5 166.9 %reduce-scatter.22.cloned.1.call-start = ((), (), s32[]{:S(2)}) async-start(), calls=%async_computation.18 | async-start | bytes 1966080 | tf_op jit(solution)/shard_map/reduce_scatter | solution.py:66
  299.7 19.7 %copy-start.12 = (bf16[192,768]{0,1:T(8,128)(2,1)S(1)}, bf16[192,768]{0,1:T(8,128)(2,1)}, u32[]{:S(2)}) copy-start(bf16[192,768]{0,1:T(8,128)(2,1)} %copy-done.11) | copy-start | bytes 884740
  331.9 95.8 %reduce-scatter.28.cloned.1.call-start = ((), (), s32[]{:S(2)}) async-start(), calls=%async_computation.21 | async-start | bytes 2654208 | tf_op jit(solution)/shard_map/reduce_scatter | solution.py:283
  337.3 42.6 %all-to-all-start.1 = ((bf16[2,3,256,256]{3,0,1,2:T(2,128)(2,1)}), bf16[2,3,256,256]{3,0,1,2:T(2,128)(2,1)S(1)}, u32[]{:S(2)}, u32[]{:S(2)}) async-start(bf16[2,3,256,256]{3,0,1,2:T(2,128)(2,1)} %copy.244), calls=%async_computation.5 | async-start | bytes 1572864 | tf_op jit(solution)/shard_map/all_to_all | solution.py:240
  340.8 125.5 %reduce-scatter.34.cloned.1.call-start = ((), (), s32[]{:S(2)}) async-start(), calls=%async_computation.24 | async-start | bytes 884736
  342.1 161.3 %reduce-scatter.36.cloned.1.call-start = ((), (), s32[]{:S(2)}) async-start(), calls=%async_computation.25 | async-start | bytes 147456
  380.1 8.5 %copy-start.2 = (bf16[512,768]{0,1:T(8,128)(2,1)S(1)}, bf16[512,768]{0,1:T(8,128)(2,1)}, u32[]{:S(2)}) copy-start(bf16[512,768]{0,1:T(8,128)(2,1)} %copy-done.1) | copy-start | bytes 2359300
  380.1 8.5 %copy-start.32 = (bf16[512,3,192]{0,2,1:T(8,128)(2,1)S(1)}, bf16[512,3,192]{0,2,1:T(8,128)(2,1)}, u32[]{:S(2)}) copy-start(bf16[512,3,192]{0,2,1:T(8,128)(2,1)} %copy-done.31) | copy-start | bytes 1769476
  388.3 160.9 %reduce-scatter.24.cloned.1.call-start = ((), (), s32[]{:S(2)}) async-start(), calls=%async_computation.19 | async-start | bytes 2654208 | tf_op jit(solution)/shard_map/reduce_scatter | solution.py:280
  390.9 195.5 %reduce-scatter.32.cloned.1.call-start = ((), (), s32[]{:S(2)}) async-start(), calls=%async_computation.23 | async-start | bytes 147456 | tf_op jit(solution)/shard_map/reduce_scatter | solution.py:286
  405.3 238.1 %reduce-scatter.26.cloned.1.call-start = ((), (), s32[]{:S(2)}) async-start(), calls=%async_computation.20 | async-start | bytes 5308416 | tf_op jit(solution)/shard_map/reduce_scatter | solution.py:282
  410.6 274.5 %reduce-scatter.30.cloned.1.call-start = ((), (), s32[]{:S(2)}) async-start(), calls=%async_computation.22 | async-start | bytes 1769472 | tf_op jit(solution)/shard_map/reduce_scatter | solution.py:284
  429.3 37.9 %copy-start.40 = (f32[192,96]{1,0:T(8,128)S(1)}, f32[192,96]{1,0:T(8,128)}, u32[]{:S(2)}) copy-start(f32[192,96]{1,0:T(8,128)} %param.29) | copy-start | bytes 221188
  469.7 79.5 %copy-start.30 = (f32[96,3,192]{2,0,1:T(8,128)S(1)}, f32[96,3,192]{2,0,1:T(8,128)}, u32[]{:S(2)}) copy-start(f32[96,3,192]{2,0,1:T(8,128)} %param.27) | copy-start | bytes 663556
  552.4 53.2 %copy-start.51 = (f32[32,12]{0,1:T(8,128)S(1)}, f32[32,12]{0,1:T(8,128)}, u32[]{:S(2)}) copy-start(f32[32,12]{0,1:T(8,128)} %param.37) | copy-start | bytes 4612
  552.4 53.3 %copy-start.59 = (f32[3,32,12]{1,2,0:T(8,128)S(1)}, f32[3,32,12]{1,2,0:T(8,128)}, u32[]{:S(2)}) copy-start(f32[3,32,12]{1,2,0:T(8,128)} %param.38) | copy-start | bytes 13828
  552.4 54.5 %copy-start.45 = (f32[43,32]{0,1:T(8,128)S(1)}, f32[43,32]{0,1:T(8,128)}, u32[]{:S(2)}) copy-start(f32[43,32]{0,1:T(8,128)} %param.39) | copy-start | bytes 16516
  552.4 54.5 %copy-start.46 = (f32[3,43,32]{1,2,0:T(8,128)S(1)}, f32[3,43,32]{1,2,0:T(8,128)}, u32[]{:S(2)}) copy-start(f32[3,43,32]{1,2,0:T(8,128)} %param.40) | copy-start | bytes 49540
  552.4 55.8 %copy-start.8 = (f32[512,192]{0,1:T(8,128)S(1)}, f32[512,192]{0,1:T(8,128)}, u32[]{:S(2)}) copy-start(f32[512,192]{0,1:T(8,128)} %copy-done.7) | copy-start | bytes 1179652
  554.5 88.9 %copy-start.14 = (f32[1,96,2,768]{3,2,1,0:T(2,128)S(1)}, f32[1,96,2,768]{3,2,1,0:T(2,128)}, u32[]{:S(2)}) copy-start(f32[1,96,2,768]{3,2,1,0:T(2,128)} %get-tuple-element.144) | copy-start | bytes 1769476
  554.5 88.9 %copy-start.15 = (f32[1,96,2,768]{3,2,1,0:T(2,128)S(1)}, f32[1,96,2,768]{3,2,1,0:T(2,128)}, u32[]{:S(2)}) copy-start(f32[1,96,2,768]{3,2,1,0:T(2,128)} %get-tuple-element.145) | copy-start | bytes 1769476
  647.3 37.8 %copy-start.35 = (f32[32,6,192]{2,0,1:T(8,128)S(1)}, f32[32,6,192]{2,0,1:T(8,128)}, u32[]{:S(2)}) copy-start(f32[32,6,192]{2,0,1:T(8,128)} %param.35) | copy-start | bytes 442372
  647.3 37.8 %copy-start.39 = (f32[3,32,6,192]{3,1,2,0:T(8,128)S(1)}, f32[3,32,6,192]{3,1,2,0:T(8,128)}, u32[]{:S(2)}) copy-start(f32[3,32,6,192]{3,1,2,0:T(8,128)} %param.36) | copy-start | bytes 1327108
  (35 other events, 85.4 us)
Sparse Core Ops, SparseCore 0:
  129.5 34.1 reduce-scatter.15
  224.0 36.2 reduce-scatter.19
  262.6 34.2 reduce-scatter.17
  332.0 48.4 reduce-scatter.21
  384.3 43.3 reduce-scatter.27
  431.3 34.9 reduce-scatter.33
  469.8 33.5 reduce-scatter.35
  506.8 42.3 reduce-scatter.23
  552.8 33.5 reduce-scatter.31
  589.7 53.7 reduce-scatter.25
  646.7 38.3 reduce-scatter.29
Sparse Core Ops, SparseCore 1:
  132.3 27.4 all-gather.3
  162.1 23.8 all-gather.5
where the time goes:
time: 705 us; the launch traced here: 695 us
  waiting for transfers between devices  347 us (49%)
  blocking collectives  173 us (25%)
  matrix products  71.1 us (10%)
  local copies, waits for them, and re-layouts  44.7 us (6%)
  other arithmetic  33 us (5%)
  between operations  16.6 us (2%)
  starting transfers between devices  9.22 us (1%)
    unnamed x15, waiting for transfers between devices  61.2 us
    reduce_scatter x2, waiting for transfers between devices, branch_total(): lax.psum_scatter(partial_value, 'mp', scatter_dimension=1, tiled=True)  55.8 us
    reduce_scatter x1, waiting for transfers between devices, local(): lax.psum_scatter(attend_grad, 'dp', scatter_dimension=0, tiled=True)  44.9 us
    all_to_all x1, waiting for transfers between devices, local(): lax.all_to_all(score_grad, 'mp', split_axis=2, concat_axis=1, tiled=True)  37.7 us
    reduce_scatter x1, waiting for transfers between devices, local(): lax.psum_scatter(modulate_grad, 'dp', scatter_dimension=0, tiled=True)  35.9 us
    all_gather x2, blocking collectives, gather_grad(): return lax.all_gather(value, 'mp', axis=1, tiled=True)  35.4 us
    all_gather x2, blocking collectives, normalize(): return (normed, spread, lax.all_gather(rows, 'mp', axis=1, tiled=True))  34.5 us
    reduce_scatter x1, waiting for transfers between devices, local(): lax.psum_scatter(expand_grad, 'dp', scatter_dimension=0, tiled=True)  33.4 us
  transfers between devices with their start and end apart: 15, of which 11 were waited for; matrix products, arithmetic and copies ran while one was open for 14% of the time, Pallas kernels for 0%

commit v1 on v0

--- a/solution.py
+++ b/solution.py
@@ -4,6 +4,8 @@
 import jax.numpy as jnp
 import numpy as np
 from jax import lax
+from jax.experimental import pallas as pl
+from jax.experimental.pallas import tpu as pltpu
 from jax.sharding import PartitionSpec as P
 
 D = 768
@@ -338,7 +340,841 @@
     )
 
 
+RATES = (
+    2.0 / math.sqrt(D),
+    2.0 / math.sqrt(D // 8),
+    2.0 / math.sqrt(D),
+    2.0 / math.sqrt(FF),
+    2.0 / math.sqrt(CDIM),
+    2.0 / math.sqrt(PAIR),
+    2.0,
+)
+f32 = jnp.float32
+bf16 = jnp.bfloat16
+NT = (((1,), (1,)), ((), ()))
+NN = (((1,), (0,)), ((), ()))
+TN = (((0,), (0,)), ((), ()))
+HEADS = 12
+GROUP = 16
+UNIT = 64
+CHUNK = 16
+PAIRS = 8
+
+
+def mm(a, b, dims=NN, precision=None):
+    return lax.dot_general(a, b, dims, precision=precision, preferred_element_type=f32)
+
+
+def head_mask(count):
+    row = lax.broadcasted_iota(jnp.int32, (count, GROUP, D), 1)
+    col = lax.broadcasted_iota(jnp.int32, (count, GROUP, D), 2) // HD
+    return row == col
+
+
+def spread_heads(rows):
+    count = rows.shape[0]
+    wide = jnp.broadcast_to(rows.astype(f32)[:, None, :], (count, GROUP, D))
+    return jnp.where(head_mask(count), wide, 0.0).astype(bf16).reshape(count * GROUP, D)
+
+
+def merge_heads(wide):
+    count = wide.shape[0] // GROUP
+    return jnp.sum(jnp.where(head_mask(count), wide.reshape(count, GROUP, D), 0.0), axis=1)
+
+
+class Net:
+    def __init__(self, send_sems, recv_sems):
+        self.d = lax.axis_index("dp")
+        self.m = lax.axis_index("mp")
+        core = self.d % 2
+        x = (self.d // 2) % 2
+        y = self.d // 4
+        self.core = core
+        self.chip = self.d // 2
+        self.chips = [self.chip, y * 2 + 1 - x, (1 - y) * 2 + x, (1 - y) * 2 + 1 - x]
+        self.partner = self.chip * 2 + 1 - core
+        self.send_sems = send_sems
+        self.recv_sems = recv_sems
+        self.sent = []
+        self.open = []
+        self.base = 0
+
+    def z(self, t):
+        return (self.m + t) % 4
+
+    def peer(self, r):
+        return self.chips[r] * 2 + self.core
+
+    def sems(self, count):
+        base = self.base
+        self.base = base + count
+        return base
+
+    def barrier(self):
+        sem = pltpu.get_barrier_semaphore()
+        targets = [(self.d, self.z(t)) for t in (1, 2, 3)]
+        targets += [(self.peer(r), self.m) for r in (1, 2, 3)] + [(self.partner, self.m)]
+        for target in targets:
+            pl.semaphore_signal(
+                sem, inc=1, device_id=target, device_id_type=pl.DeviceIdType.MESH
+            )
+        pl.semaphore_wait(sem, len(targets))
+
+    def copy(self, src, dst, recv, target, send=None):
+        send = len(self.sent) if send is None else send
+        return pltpu.make_async_remote_copy(
+            src_ref=src,
+            dst_ref=dst,
+            send_sem=self.send_sems.at[send],
+            recv_sem=self.recv_sems.at[recv],
+            device_id=target,
+            device_id_type=pl.DeviceIdType.MESH,
+        )
+
+    def send(self, src, dst, recv, target):
+        made = self.copy(src, dst, recv, target)
+        made.start()
+        self.sent.append(made)
+        self.open.append(made)
+        return made
+
+    def wait(self, dst, recv):
+        self.copy(dst, dst, recv, (self.partner, self.m), 0).wait_recv()
+
+    def drain(self):
+        for made in self.open:
+            made.wait_send()
+
+    def settle(self, made):
+        made.wait_send()
+        self.open = [other for other in self.open if other is not made]
+
+
+class Spread:
+    def __init__(self, net, slot):
+        self.net, self.slot, self.base = net, slot, net.sems(7)
+
+    def start(self, src=None):
+        net = self.net
+        own = self.slot(net.d)
+        src = own if src is None else src
+        for r in (1, 2, 3):
+            net.send(src, own, self.base + r, (net.peer(r), net.m))
+        net.send(src, own, self.base, (net.partner, net.m))
+
+    def forward(self, r):
+        net = self.net
+        slot = self.slot(net.peer(r))
+        net.wait(slot, self.base + r)
+        return net.send(slot, slot, self.base + 3 + r, (net.partner, net.m))
+
+    def finish(self):
+        net = self.net
+        net.wait(self.slot(net.partner), self.base)
+        for r in (1, 2, 3):
+            net.wait(self.slot(net.chips[r] * 2 + 1 - net.core), self.base + 3 + r)
+
+
+class Zline:
+    def __init__(self, net, slot):
+        self.net, self.slot, self.base = net, slot, net.sems(4)
+
+    def send(self, t, src):
+        net = self.net
+        net.send(src, self.slot(net.m), self.base + net.m, (net.d, net.z(t)))
+
+    def wait(self, t):
+        net = self.net
+        source = net.z(t)
+        net.wait(self.slot(source), self.base + source)
+        return source
+
+
+def layer_kernel(
+    ms, am, es, xp, gp, pair, sinus, pick, mask,
+    out_o, res_o, ds_o, pw_o, am_o, es_o, mod_o, pc_o,
+    msg, amg, esg, xg, gg, modu, modg, modf, bpg, pb, bias, n1, sp1, r1,
+    kf, vf, qf, pr, mix, att, mid, n2, sp2, r2, fg, act, upg, fp, fl, p2, p2l, p2o, fpo,
+    esp, epl, exl, eso, dkv, dkf, dvf, dqf, mgd, l2, rhs2, p1, p1l,
+    amp, axl, aso, azs, azl, mps, mpl, mrg, pws, pwl, pwx, pwy, pco, pcl,
+    ops, opl, rps, rpl, ctf, cfull,
+    send_sems, recv_sems, pair_sems,
+):
+    net = Net(send_sems, recv_sems)
+    d, m = net.d, net.m
+    net.barrier()
+
+    chunks = 16
+    slots = pb.shape[0]
+
+    def pair_copy(step):
+        c = step % chunks
+        return pltpu.make_async_copy(
+            pair.at[c // 8, pl.ds((c % 8) * PAIRS, PAIRS)],
+            pb.at[step % slots],
+            pair_sems.at[step % slots],
+        )
+
+    for step in range(slots):
+        pair_copy(step).start()
+
+    ms_all = Spread(net, lambda i: msg.at[i])
+    am_line = Zline(net, lambda s: amg.at[s, d])
+    am_all = [Spread(net, lambda i, t=t: amg.at[net.z(t), i]) for t in range(4)]
+    x_line = Zline(net, lambda s: xg.at[s])
+    g_line = Zline(net, lambda s: gg.at[s])
+    mod_line = Zline(net, lambda s: modg.at[s])
+    bp_all = Spread(net, lambda i: bpg.at[i])
+    es_all = Spread(net, lambda i: esg.at[i])
+
+    ms_all.start(ms)
+    for t in (1, 2, 3):
+        am_line.send(t, am)
+    am_all[0].start(am)
+    for t in (1, 2, 3):
+        x_line.send(t, xp)
+    msg[d] = ms[...]
+    amg[m, d] = am[...]
+    esg[d] = es[...]
+    xg[m] = xp[...]
+    gg[m] = gp[...]
+    for r in (1, 2, 3):
+        ms_all.forward(r)
+    ms_all.finish()
+
+    slab = msg[:, :, 0:128].reshape(256, 128)
+    select = (
+        lax.broadcasted_iota(jnp.int32, (GROUP, 128), 1)
+        == lax.broadcasted_iota(jnp.int32, (GROUP, 128), 0) + 64
+    ) & (lax.broadcasted_iota(jnp.int32, (GROUP, 128), 0) < HEADS)
+    pw_o[...] = mm(jnp.where(select, 1.0, 0.0).astype(bf16), slab, NT).astype(bf16)
+    before = sinus[...] + mm(pick[...], slab, NT)
+    condition = (before * jax.nn.sigmoid(before)).astype(bf16)
+    modu[...] = mm(condition, msg[:, :, 128:1280].reshape(256, 1152))
+    for t in (1, 2, 3):
+        mod_line.send(t, modu)
+    modg[m] = modu[...]
+    bpg[d] = jnp.concatenate([before, pick[...].astype(f32)], axis=-1)
+
+    def bias_chunk(step):
+        slot = step % slots
+        pair_copy(step).wait()
+
+        def one(i, carry):
+            part = mm(pw_o[...], pb[slot, i], NT)
+            at = pl.multiple_of((step % 8) * PAIRS * GROUP + i * GROUP, GROUP)
+            bias[step // 8, pl.ds(at, GROUP), :] = part.astype(bf16)
+            return carry
+
+        lax.fori_loop(0, PAIRS, one, 0, unroll=4)
+        pair_copy(step + slots).start()
+
+    for step in range(4):
+        bias_chunk(step)
+    for t in (1, 3, 2):
+        am_line.wait(t)
+        am_all[t].start()
+        first = {1: 4, 3: 6, 2: 8}[t]
+        bias_chunk(first)
+        bias_chunk(first + 1)
+    for r in (1, 2, 3):
+        am_all[0].forward(r)
+    es_all.start(es)
+    for t in (1, 2, 3):
+        g_line.send(t, gp)
+    bp_all.start()
+    bias_chunk(10)
+    bias_chunk(11)
+    for r in (1, 2, 3):
+        am_all[1].forward(r)
+    for step in range(12, 16):
+        bias_chunk(step)
+
+    for t in (1, 2, 3):
+        mod_line.wait(t)
+    for j in range(6):
+        modf[j] = jnp.concatenate([modg[s, :, 192 * j : 192 * j + 192] for s in range(4)], axis=-1)
+    for t in (1, 2, 3):
+        x_line.wait(t)
+
+    def unpack(ref, w, unit):
+        parts = []
+        for s in range(4):
+            parts.append(ref[s, pl.ds(w * 256 + unit * UNIT, UNIT), :].astype(f32))
+            low = ref[s, pl.ds(512 + unit * UNIT, UNIT), :].astype(f32)
+            parts.append(low[:, 64 * w : 64 * w + 64])
+        return jnp.concatenate(parts, axis=-1)
+
+    def norm(v):
+        center = jnp.mean(v, axis=-1, keepdims=True)
+        spread = lax.rsqrt(jnp.mean(v * v, axis=-1, keepdims=True) - center * center + NORM_EPS)
+        return (v - center) * spread, spread
+
+    for w in range(2):
+
+        def first_norm(unit, carry, w=w):
+            v = unpack(xg, w, unit)
+            rows = pl.ds(pl.multiple_of(w * 256 + unit * UNIT, UNIT), UNIT)
+            normed, spread = norm(v)
+            n1[rows, :] = normed
+            sp1[rows, :] = jnp.broadcast_to(spread, (UNIT, 128))
+            shift = modf[0, pl.ds(w * 4 + unit, 1), :]
+            scale = modf[1, pl.ds(w * 4 + unit, 1), :]
+            r1[rows, :] = (normed * (1.0 + scale) + shift).astype(bf16)
+            return carry
+
+        lax.fori_loop(0, 4, first_norm, 0)
+
+    for t in (3, 2):
+        for r in (1, 2, 3):
+            am_all[t].forward(r)
+    for t in (0, 1, 3, 2):
+        am_all[t].finish()
+
+    def own(w):
+        return pl.ds(pl.multiple_of(w * 256 + m * UNIT, UNIT), UNIT)
+
+    def weight(s, lo, hi):
+        return amg[s, :, :, lo:hi].reshape(D, hi - lo)
+
+    r1_own = jnp.concatenate([r1[own(0), :], r1[own(1), :]], axis=0)
+    qf[...] = jnp.concatenate(
+        [mm(r1_own, weight(s, 384, 768))[:, 0:192] for s in range(4)], axis=-1
+    ).astype(bf16)
+    for w in range(2):
+        rows = slice(w * 256, w * 256 + 256)
+        both = [mm(r1[rows, :], weight(s, 0, 384)) for s in range(4)]
+        kf[rows, :] = jnp.concatenate([v[:, 0:192] for v in both], axis=-1).astype(bf16)
+        vf[rows, :] = jnp.concatenate([v[:, 192:384] for v in both], axis=-1).astype(bf16)
+
+    factor = HD ** (-0.5)
+
+    def attend(c, carry):
+        w = c // 4
+        mine = pl.ds(pl.multiple_of(c * CHUNK, CHUNK), CHUNK)
+        keys = pl.ds(pl.multiple_of(w * 256, 256), 256)
+        wide = pl.ds(pl.multiple_of((c % 4) * CHUNK * GROUP, CHUNK * GROUP), CHUNK * GROUP)
+        scores = mm(spread_heads(qf[mine, :]), kf[keys, :], NT) * factor
+        scores = scores + bias[w, wide, :].astype(f32) + mask[pl.ds(w, 1), :]
+        peak = jnp.max(scores, axis=-1, keepdims=True)
+        expo = jnp.exp(scores - peak)
+        chance = expo / jnp.sum(expo, axis=-1, keepdims=True)
+        pr[w, wide, :] = chance
+        mix[mine, :] = merge_heads(mm(chance.astype(bf16), vf[keys, :])).astype(bf16)
+        return carry
+
+    lax.fori_loop(0, 8, attend, 0)
+    es_sent = [es_all.forward(r) for r in (1, 2, 3)]
+
+    mixed = mix[...]
+    blank = jnp.zeros((128, 192), bf16)
+    attended = mm(
+        jnp.concatenate([blank, mixed[:, 0:192]], axis=-1), weight(0, 384, 768), NT
+    )
+    for s in range(1, 4):
+        part = jnp.concatenate([blank, mixed[:, 192 * s : 192 * s + 192]], axis=-1)
+        attended = attended + mm(part, weight(s, 384, 768), NT)
+    att[...] = attended
+
+    def mod_row(j, w):
+        return modf[j, pl.ds(w * 4 + m, 1), :]
+
+    for w in range(2):
+        half = slice(w * UNIT, w * UNIT + UNIT)
+        middle = unpack(xg, w, m) + mod_row(2, w) * att[half, :]
+        mid[half, :] = middle
+        normed, spread = norm(middle)
+        n2[half, :] = normed
+        sp2[half, :] = jnp.broadcast_to(spread, (UNIT, 128))
+        r2[m, half, :] = (normed * (1.0 + mod_row(4, w)) + mod_row(3, w)).astype(bf16)
+
+    r2_line = Zline(net, lambda s: r2.at[s])
+    for t in (1, 3, 2):
+        r2_line.send(t, r2.at[m])
+    for t in (1, 2, 3):
+        g_line.wait(t)
+    for s in range(4):
+        for w in range(2):
+            half = slice(w * UNIT, w * UNIT + UNIT)
+            upper = unpack(gg, w, s)
+            fg[s, half, :] = (modf[5, w * 4 + s : w * 4 + s + 1, :] * upper).astype(bf16)
+    es_all.finish()
+
+    p2_line = Zline(net, lambda s: p2l.at[s])
+    f_line = Zline(net, lambda s: fl.at[s])
+
+    def feed(s):
+        expand = esg[:, :, 0:1536].reshape(D, 1536)
+        shrink = esg[:, :, 1536:2304].reshape(D, 768)
+        up = mm(r2[s], expand)
+        gate = up[:, 0:768]
+        upward = up[:, 768:1536]
+        act_grad = mm(fg[s], shrink)
+        sigma = jax.nn.sigmoid(gate)
+        activated = (gate * sigma * upward).astype(bf16)
+        act[s] = activated
+        slope = sigma * (1.0 + gate * (1.0 - sigma))
+        grads = jnp.concatenate(
+            [(act_grad * upward * slope).astype(bf16), (act_grad * gate * sigma).astype(bf16)],
+            axis=-1,
+        )
+        upg[s] = grads
+        return mm(grads, expand, NT), mm(activated, shrink, NT)
+
+    partial, fed = feed(m)
+    p2o[...] = partial
+    fpo[...] = fed
+    for t in (1, 3, 2):
+        source = r2_line.wait(t)
+        partial, fed = feed(source)
+        p2[source] = partial.astype(bf16)
+        p2_line.send(t, p2.at[source])
+        fp[source] = fed.astype(bf16)
+    for t in (1, 3, 2):
+        f_line.send(t, fp.at[net.z(t)])
+
+    def put_es(left, right, at):
+        for h in range(2):
+            value = mm(left[:, :, 384 * h : 384 * h + 384].reshape(512, 384), right, TN)
+            for i in range(4):
+                part = value[96 * i : 96 * i + 96, :].astype(bf16)
+                esp[i % 2, 2 * h + i // 2, :, at : at + 768] = part
+
+    put_es(r2, upg[:, :, 0:768].reshape(512, 768), 0)
+    put_es(r2, upg[:, :, 768:1536].reshape(512, 768), 768)
+    put_es(fg, act[...].reshape(512, 768), 1536)
+    for made in es_sent:
+        net.settle(made)
+    es_pair = net.sems(1)
+    net.send(esp.at[1 - net.core], epl, es_pair, (net.partner, m))
+
+    for t in (1, 3, 2):
+        p2_line.wait(t)
+
+    def norm_back(upstream, normed, spread, scale):
+        inner = upstream * (1.0 + scale)
+        first = jnp.mean(inner, axis=-1, keepdims=True)
+        second = jnp.mean(inner * normed, axis=-1, keepdims=True)
+        return spread * (inner - first - normed * second)
+
+    def unit_sum(v):
+        return jnp.sum(v, axis=0, keepdims=True)
+
+    own_sums = [[None] * 6, [None] * 6]
+    for w in range(2):
+        half = slice(w * UNIT, w * UNIT + UNIT)
+        upstream = p2o[half, :]
+        for t in (1, 3, 2):
+            upstream = upstream + p2l[net.z(t), half, :].astype(f32)
+        normed = n2[half, :]
+        back = norm_back(upstream, normed, sp2[half, 0:1], mod_row(4, w))
+        grad = unpack(gg, w, m) + back
+        p2o[half, :] = grad
+        own_sums[w][2] = unit_sum(grad * att[half, :])
+        own_sums[w][3] = unit_sum(upstream)
+        own_sums[w][4] = unit_sum(upstream * normed)
+        l2[slice(128 + w * UNIT, 128 + w * UNIT + UNIT), :] = (mod_row(2, w) * grad).astype(bf16)
+        l2[half, :] = r1[own(w), :]
+    merged_grad = l2[128:256, :]
+    mgd[...] = jnp.concatenate(
+        [mm(merged_grad, weight(s, 384, 768))[:, 192:384] for s in range(4)], axis=-1
+    ).astype(bf16)
+
+    net.wait(epl, es_pair)
+    es_chip = net.sems(4)
+    for r in (1, 2, 3, 0):
+        total = esp[net.core, net.chips[r]].astype(f32) + epl[net.chips[r]].astype(f32)
+        if r == 0:
+            eso[...] = total
+        else:
+            esp[net.core, net.chips[r]] = total.astype(bf16)
+            net.send(
+                esp.at[net.core, net.chips[r]], exl.at[r - 1], es_chip + r, (net.peer(r), m)
+            )
+
+    dkf[...] = jnp.zeros_like(dkf)
+    dvf[...] = jnp.zeros_like(dvf)
+
+    def attend_back(c, carry):
+        w = c // 4
+        mine = pl.ds(pl.multiple_of(c * CHUNK, CHUNK), CHUNK)
+        keys = pl.ds(pl.multiple_of(w * 256, 256), 256)
+        wide = pl.ds(pl.multiple_of((c % 4) * CHUNK * GROUP, CHUNK * GROUP), CHUNK * GROUP)
+        grad = spread_heads(mgd[mine, :])
+        chance = pr[w, wide, :]
+        chance_grad = mm(grad, vf[keys, :], NT)
+        inner = jnp.sum(chance * chance_grad, axis=-1, keepdims=True)
+        score = (chance * (chance_grad - inner)).astype(bf16)
+        ds_o[w, wide, :] = score
+        dqf[mine, :] = (merge_heads(mm(score, kf[keys, :])) * factor).astype(bf16)
+        dvf[keys, :] += mm(chance.astype(bf16), grad, TN)
+        dkf[keys, :] += mm(score, spread_heads(qf[mine, :]), TN) * factor
+        return carry
+
+    lax.fori_loop(0, 8, attend_back, 0)
+
+    o_line = Zline(net, lambda s: opl.at[s])
+
+    def pack(line, value, ref):
+        for s in range(4):
+            part = value[:, 192 * s : 192 * s + 192]
+            ref[s, 0:128, :] = part[:, 0:128].astype(bf16)
+            low = part[:, 128:192]
+            ref[s, 128:192, :] = jnp.concatenate([low[0:64], low[64:128]], axis=-1).astype(bf16)
+        for t in (1, 3, 2):
+            line.send(t, ref.at[net.z(t)])
+
+    def unpack_out(line, ref, mine, to):
+        for t in (0, 1, 3, 2):
+            s = net.z(t)
+            block = mine if t == 0 else ref
+            if t:
+                line.wait(t)
+            for w in range(2):
+                rows = pl.ds(pl.multiple_of(w * 256 + s * UNIT, UNIT), UNIT)
+                high = block[s, w * UNIT : w * UNIT + UNIT, :].astype(f32)
+                low = block[s, 128:192, :].astype(f32)[:, 64 * w : 64 * w + 64]
+                to[rows, :] = jnp.concatenate([high, low], axis=-1).astype(bf16)
+
+    for t in (1, 3, 2):
+        f_line.wait(t)
+    done = []
+    for w in range(2):
+        half = slice(w * UNIT, w * UNIT + UNIT)
+        fed = fpo[half, :]
+        for t in (1, 3, 2):
+            fed = fed + fl[net.z(t), half, :].astype(f32)
+        own_sums[w][5] = unit_sum(unpack(gg, w, m) * fed)
+        done.append(mid[half, :] + mod_row(5, w) * fed)
+    pack(o_line, jnp.concatenate(done, axis=0), ops)
+
+    for s in range(4):
+        cols = slice(192 * s, 192 * s + 192)
+        dkv[s] = jnp.concatenate([dkf[:, cols], dvf[:, cols]], axis=-1).astype(bf16)
+        rhs2[s, 0:128, :] = jnp.concatenate([dqf[:, cols], blank], axis=-1)
+        rhs2[s, 128:256, :] = jnp.concatenate([blank, mix[:, cols]], axis=-1)
+    am_pair = net.sems(4)
+
+    def apl(t):
+        return esg.at[pl.ds(4 * (t // 3), 4), :, 768 * (t % 3) : 768 * (t % 3) + 768]
+
+    for t in (1, 3, 2, 0):
+        s = net.z(t)
+        for h in range(2):
+            cols = slice(384 * h, 384 * h + 384)
+            for left, right, at in ((r1, dkv, 0), (l2, rhs2, 384)):
+                value = mm(left[:, cols], right[s], TN)
+                for i in range(4):
+                    part = value[96 * i : 96 * i + 96, :].astype(bf16)
+                    amp[s, i % 2, 2 * h + i // 2, :, at : at + 384] = part
+        net.send(amp.at[s, 1 - net.core], apl(t), am_pair + t, (net.partner, m))
+
+    for w in range(2):
+        rows = slice(w * 256, w * 256 + 256)
+        total = mm(dkv[0, rows, :], weight(0, 0, 384), NT)
+        for s in range(1, 4):
+            total = total + mm(dkv[s, rows, :], weight(s, 0, 384), NT)
+        dkf[rows, :] = total
+    total = mm(rhs2[0, 0:128, :], weight(0, 384, 768), NT)
+    for s in range(1, 4):
+        total = total + mm(rhs2[s, 0:128, :], weight(s, 384, 768), NT)
+    for w in range(2):
+        dkf[own(w), :] += total[w * UNIT : w * UNIT + UNIT, :]
+    p1_line = Zline(net, lambda s: p1l.at[s])
+    for t in (1, 3, 2):
+        s = net.z(t)
+        for w in range(2):
+            rows = pl.ds(pl.multiple_of(w * 256 + s * UNIT, UNIT), UNIT)
+            p1[s, w * UNIT : w * UNIT + UNIT, :] = dkf[rows, :].astype(bf16)
+        p1_line.send(t, p1.at[s])
+
+    sums = [[], []]
+    for u in range(8):
+        rows = slice(u * UNIT, u * UNIT + UNIT)
+        sums[0].append(unit_sum(dkf[rows, :]))
+        sums[1].append(unit_sum(dkf[rows, :] * n1[rows, :]))
+    row = lax.broadcasted_iota(jnp.int32, (8, D), 0)
+    table = [jnp.concatenate(sums[0], axis=0), jnp.concatenate(sums[1], axis=0)]
+    for j in range(2, 6):
+        first = jnp.broadcast_to(own_sums[0][j], (8, D))
+        second = jnp.broadcast_to(own_sums[1][j], (8, D))
+        table.append(jnp.where(row == m, first, jnp.where(row == m + 4, second, 0.0)))
+    mod_sum = Zline(net, lambda s: mpl.at[s])
+    for s in range(4):
+        mps[s] = jnp.concatenate([v[:, 192 * s : 192 * s + 192] for v in table], axis=-1)
+    for t in (1, 3, 2):
+        mod_sum.send(t, mps.at[net.z(t)])
+
+    def pair_chunk(step, acc):
+        slot = step % slots
+        pair_copy(step).wait()
+
+        def one(i, acc):
+            at = pl.multiple_of((step % 8) * PAIRS * GROUP + i * GROUP, GROUP)
+            return acc + mm(ds_o[(step - 16) // 8, pl.ds(at, GROUP), :], pb[slot, i])
+
+        acc = lax.fori_loop(0, PAIRS, one, acc, unroll=4)
+        if step + slots < 2 * chunks:
+            pair_copy(step + slots).start()
+        return acc
+
+    pairwise = jnp.zeros((GROUP, 256), f32)
+    am_chip = net.sems(16)
+    step = 16
+    for t in (1, 3, 2, 0):
+        s = net.z(t)
+        net.wait(apl(t), am_pair + t)
+        base, cols = 4 * (t // 3), slice(768 * (t % 3), 768 * (t % 3) + 768)
+        for r in (1, 2, 3, 0):
+            total = amp[s, net.core, net.chips[r]].astype(f32)
+            total = total + esg[base + net.chips[r], :, cols].astype(f32)
+            if r == 0:
+                aso[s] = total
+            else:
+                amp[s, net.core, net.chips[r]] = total.astype(bf16)
+                net.send(
+                    amp.at[s, net.core, net.chips[r]],
+                    axl.at[s, r - 1],
+                    am_chip + 4 * t + r,
+                    (net.peer(r), m),
+                )
+        for _ in range(4):
+            pairwise = pair_chunk(step, pairwise)
+            step += 1
+
+    for r in (1, 2, 3):
+        bp_all.forward(r)
+    bp_all.finish()
+
+    wide = jnp.concatenate([pairwise, jnp.zeros((112, 256), f32)], axis=0).T
+    for i in range(8):
+        pws[i % 2, i // 2] = wide[32 * i : 32 * i + 32, :]
+    pw_pair = net.sems(1)
+    net.send(pws.at[1 - net.core], pwl, pw_pair, (net.partner, m))
+
+    for t in (1, 3, 2):
+        mod_sum.wait(t)
+    mod_grad = mps[m]
+    for t in (1, 3, 2):
+        mod_grad = mod_grad + mpl[net.z(t)]
+    mrg[d] = mod_grad
+    mr_all = Spread(net, lambda i: mrg.at[i])
+    mr_all.start()
+
+    for t in (1, 3, 2):
+        p1_line.wait(t)
+    r_line = Zline(net, lambda s: rpl.at[s])
+    done = []
+    for w in range(2):
+        half = slice(w * UNIT, w * UNIT + UNIT)
+        upstream = dkf[own(w), :]
+        for t in (1, 3, 2):
+            upstream = upstream + p1l[net.z(t), half, :].astype(f32)
+        back = norm_back(upstream, n1[own(w), :], sp1[own(w), :][:, 0:1], mod_row(1, w))
+        done.append(p2o[half, :] + back)
+    pack(r_line, jnp.concatenate(done, axis=0), rps)
+
+    total = eso[...]
+    for r in (1, 2, 3):
+        net.wait(exl.at[r - 1], es_chip + r)
+        total = total + exl[r - 1].astype(f32)
+    es_o[...] = total
+
+    net.wait(pwl, pw_pair)
+    pw_chip = net.sems(4)
+    for r in (1, 2, 3):
+        pwx[r] = pws[net.core, net.chips[r]] + pwl[net.chips[r]]
+        net.send(pwx.at[r], pwy.at[r], pw_chip + r, (net.peer(r), m))
+    pair_sum = pws[net.core, net.chip] + pwl[net.chip]
+
+    am_z = Zline(net, lambda s: azl.at[s])
+    for t in (1, 3, 2, 0):
+        s = net.z(t)
+        total = aso[s]
+        for r in (1, 2, 3):
+            net.wait(axl.at[s, r - 1], am_chip + 4 * t + r)
+            total = total + axl[s, r - 1].astype(f32)
+        if t:
+            azs[s] = total.astype(bf16)
+            am_z.send(t, azs.at[s])
+        else:
+            aso[s] = total
+        if t == 1:
+            for r in (1, 2, 3):
+                mr_all.forward(r)
+
+    mr_all.finish()
+    before = bpg[:, :, 0:256].reshape(64, 256)
+    sig = jax.nn.sigmoid(before)
+    condition = (before * sig).astype(bf16).astype(f32)
+    picks = bpg[:, :, 256:384].reshape(64, 128)
+    grads = mrg[...].reshape(64, 1152)
+    ctf[...] = condition.T
+    mod_o[...] = mm(ctf[pl.ds(pl.multiple_of(d * 32, 32), 32), :], grads, NN, HIGH)
+    cond_grad = mm(grads, msg[:, :, 128:1280].reshape(256, 1152).astype(f32), NT, HIGH)
+    before_grad = cond_grad * (sig * (1.0 + before * (1.0 - sig)))
+    cfull[...] = mm(before_grad, picks, TN, HIGH)
+    for r in (1, 2, 3):
+        net.wait(pwy.at[r], pw_chip + r)
+        pair_sum = pair_sum + pwy[r]
+    pco[...] = jnp.concatenate(
+        [pair_sum, cfull[pl.ds(pl.multiple_of(d * 32, 32), 32), :]], axis=-1
+    )
+    pc_line = Zline(net, lambda s: pcl.at[s])
+    for t in (1, 3, 2):
+        pc_line.send(t, pco)
+
+    unpack_out(o_line, opl, ops, out_o)
+    unpack_out(r_line, rpl, rps, res_o)
+    total = aso[m]
+    for t in (1, 3, 2):
+        total = total + azl[am_z.wait(t)].astype(f32)
+    am_o[...] = total
+    total = pco[...]
+    for t in (1, 3, 2):
+        total = total + pcl[pc_line.wait(t)]
+    pc_o[...] = total
+    net.drain()
+
+
+def layer_call(*args):
+    V = pltpu.VMEM
+    scratch = [
+        V((8, 32, 1280), bf16), V((4, 8, 96, 768), bf16), V((8, 96, 2304), bf16),
+        V((4, 768, 128), bf16), V((4, 768, 128), bf16),
+        V((8, 1152), f32), V((4, 8, 1152), f32), V((6, 8, 768), f32), V((8, 8, 384), f32),
+        V((2, PAIRS, 256, 256), bf16), V((2, 1024, 256), bf16),
+        V((512, 768), f32), V((512, 128), f32), V((512, 768), bf16),
+        V((512, 768), bf16), V((512, 768), bf16), V((128, 768), bf16), V((2, 1024, 256), f32),
+        V((128, 768), bf16), V((128, 768), f32), V((128, 768), f32), V((128, 768), f32),
+        V((128, 128), f32),
+        V((4, 128, 768), bf16), V((4, 128, 768), bf16), V((4, 128, 768), bf16),
+        V((4, 128, 1536), bf16), V((4, 128, 768), bf16), V((4, 128, 768), bf16),
+        V((4, 128, 768), bf16), V((4, 128, 768), bf16), V((128, 768), f32), V((128, 768), f32),
+        V((2, 4, 96, 2304), bf16), V((4, 96, 2304), bf16), V((3, 96, 2304), bf16),
+        V((96, 2304), f32),
+        V((4, 512, 384), bf16), V((512, 768), f32), V((512, 768), f32), V((128, 768), bf16),
+        V((128, 768), bf16), V((256, 768), bf16), V((4, 256, 384), bf16),
+        V((4, 128, 768), bf16), V((4, 128, 768), bf16),
+        V((4, 2, 4, 96, 768), bf16), V((4, 3, 96, 768), bf16),
+        V((4, 96, 768), f32), V((4, 96, 768), bf16), V((4, 96, 768), bf16),
+        V((4, 8, 1152), f32), V((4, 8, 1152), f32), V((8, 8, 1152), f32),
+        V((2, 4, 32, 128), f32), V((4, 32, 128), f32), V((4, 32, 128), f32), V((4, 32, 128), f32),
+        V((32, 256), f32), V((4, 32, 256), f32),
+        V((4, 192, 128), bf16), V((4, 192, 128), bf16), V((4, 192, 128), bf16),
+        V((4, 192, 128), bf16), V((256, 64), f32), V((256, 128), f32),
+        pltpu.SemaphoreType.DMA((160,)), pltpu.SemaphoreType.DMA((160,)),
+        pltpu.SemaphoreType.DMA((2,)),
+    ]
+    whole = pl.BlockSpec(memory_space=pltpu.VMEM)
+    outs = (
+        ((512, 192), bf16), ((512, 192), bf16), ((2, 1024, 256), bf16), ((16, 256), bf16),
+        ((96, 768), f32), ((96, 2304), f32), ((32, 1152), f32), ((32, 256), f32),
+    )
+    return pl.pallas_call(
+        layer_kernel,
+        out_shape=tuple(jax.ShapeDtypeStruct(s, t) for s, t in outs),
+        in_specs=[pl.BlockSpec(memory_space=pl.ANY) if i == 5 else whole for i in range(9)],
+        out_specs=(whole,) * len(outs),
+        scratch_shapes=scratch,
+        compiler_params=pltpu.CompilerParams(
+            collective_id=0, has_side_effects=True, vmem_limit_bytes=67043328
+        ),
+        name="layer",
+    )(*args)
+
+
+def pair_kernel(ds, pw, out):
+    for i in range(8):
+        out[0, i] = mm(ds[0, GROUP * i : GROUP * i + GROUP, :], pw[...], TN).astype(bf16)
+
+
+def pair_call(ds, pw):
+    return pl.pallas_call(
+        pair_kernel,
+        grid=(2, 8),
+        out_shape=jax.ShapeDtypeStruct((2, 64, 256, 256), bf16),
+        in_specs=[
+            pl.BlockSpec((1, 128, 256), lambda w, i: (w, i, 0)),
+            pl.BlockSpec((16, 256), lambda w, i: (0, 0)),
+        ],
+        out_specs=pl.BlockSpec((1, 8, 256, 256), lambda w, i: (w, i, 0, 0)),
+        name="pair",
+    )(ds, pw)
+
+
+def fast_local(
+    residues, pair_input, out_grad, bucket_layout, time_bins, fold_class,
+    attend_weight, attend_state, merge_weight, merge_state, expand_weight, expand_state,
+    shrink_weight, shrink_state, modulate_weight, modulate_state, pair_weight, pair_state,
+    class_weight, class_state,
+):
+    m = lax.axis_index("mp")
+    classes = class_weight.shape[0]
+    am = jnp.concatenate(
+        [attend_weight[:, 1], attend_weight[:, 2], attend_weight[:, 0], merge_weight.T], axis=1
+    ).astype(bf16)
+    es = jnp.concatenate(
+        [expand_weight[:, 0], expand_weight[:, 1], shrink_weight.T], axis=1
+    ).astype(bf16)
+    ms = jnp.concatenate(
+        [
+            jnp.pad(class_weight.T, ((0, 0), (0, 64 - classes))),
+            jnp.pad(pair_weight, ((0, 0), (0, 52))),
+            modulate_weight.reshape(32, 1152),
+        ],
+        axis=1,
+    ).astype(bf16)
+
+    def packed(v):
+        low = v[:, 128:]
+        return jnp.concatenate([v[:, :128], jnp.concatenate([low[:256], low[256:]], axis=1)], axis=0)
+
+    table = jnp.asarray(PATTERNS)
+    layout = (bucket_layout[:, None] == jnp.arange(5, dtype=jnp.int32)).astype(jnp.int32)
+    unit_slot = jnp.sum(layout[:, :, None] * table[None], axis=1)
+    pick_slot = (unit_slot[..., None] == jnp.arange(4, dtype=jnp.int32)).astype(jnp.int32)
+    unit_bin = jnp.sum(pick_slot * time_bins[:, None, :], axis=-1).reshape(8)
+    unit_class = jnp.sum(pick_slot * fold_class[:, None, :], axis=-1).reshape(8)
+    sinus = time_features(unit_bin, 256)
+    pick = (unit_class[:, None] == jnp.arange(128, dtype=jnp.int32)).astype(bf16)
+    mine = jnp.sum(
+        unit_slot * (jnp.arange(4, dtype=jnp.int32)[None] == m).astype(jnp.int32),
+        axis=1,
+        keepdims=True,
+    )
+    seen = jnp.where(unit_slot == mine, 0.0, MASKED)
+    mask = jnp.broadcast_to(seen[:, :, None], (2, 4, UNIT)).reshape(2, 256)
+
+    out, res, ds, pw, am_g, es_g, mod_g, pc_g = layer_call(
+        ms, am, es, packed(residues), packed(out_grad), pair_input, sinus, pick, mask
+    )
+    pair_grad = pair_call(ds, pw)
+    grads = (
+        jnp.stack([am_g[:, 384:576], am_g[:, 0:192], am_g[:, 192:384]], axis=1),
+        am_g[:, 576:768].T,
+        jnp.stack([es_g[:, 0:768], es_g[:, 768:1536]], axis=1),
+        es_g[:, 1536:2304].T,
+        mod_g.reshape(32, 6, 192),
+        pc_g[:, 0:HEADS],
+        pc_g[:, 128 : 128 + classes].T,
+    )
+    masters = (
+        attend_weight, merge_weight, expand_weight, shrink_weight, modulate_weight, pair_weight,
+        class_weight,
+    )
+    states = (
+        attend_state, merge_state, expand_state, shrink_state, modulate_state, pair_state,
+        class_state,
+    )
+    results = []
+    for master, state, grad, rate in zip(masters, states, grads, RATES):
+        results.extend(adamw(master, state, grad, rate))
+    return (out, res, pair_grad, *results)
+
+
 def solution(mesh):
+    quick = mesh.shape["dp"] == 8 and mesh.shape["mp"] == 4
     placed = (
         P("dp", "mp"),
         P("dp", "mp", None, None),
@@ -362,7 +1198,7 @@
         P(None, None, "dp"),
     )
     return jax.shard_map(
-        local,
+        fast_local if quick else local,
         mesh=mesh,
         in_specs=placed,
         out_specs=(

time: 705 us -> 225 us (0.32)
  waiting for transfers between devices: 347 us -> 0 us
  Pallas kernels: 0 us -> 187 us
  blocking collectives: 173 us -> 0 us
  matrix products: 71.1 us -> 0 us
  local copies, waits for them, and re-layouts: 44.7 us -> 18.7 us
  other arithmetic: 33 us -> 15.6 us
  between operations: 16.6 us -> 1.18 us
  starting transfers between devices: 9.22 us -> 0 us
    reduce_scatter x9 -> x0, waiting for transfers between devices: 248 us -> none  [the longest x2 55.8 us: branch_total(): lax.psum_scatter(partial_value, 'mp', scatter_dimension=1, tiled=True)]
    pallas_call x0 -> x2, Pallas kernels: none -> 187 us  [the longest x1 173 us: layer_call(): pl.pallas_call(layer_kernel, out_shape=tuple((jax.ShapeDtypeStruct(s, t)...]
    all_gather x9 -> x0, blocking collectives: 122 us -> none  [the longest x2 35.4 us: gather_grad(): return lax.all_gather(value, 'mp', axis=1, tiled=True)]
    dot_general x27 -> x0, matrix products: 67.7 us -> none  [the longest x1 10.2 us: local(): jnp.einsum('wijc,ch->whij', pair_input, pair_full, preferred_element_type...]
    unnamed x15 -> x0, waiting for transfers between devices: 61.2 us -> none
    psum x4 -> x0, blocking collectives: 51.7 us -> none  [the longest x2 29 us: normalize_back(): lax.psum((jnp.sum(inner, axis=1), jnp.sum(inner * normed, axis=1)), 'mp')]
    all_to_all x2 -> x0, waiting for transfers between devices: 37.7 us -> none  [the longest x1 37.7 us: local(): lax.all_to_all(score_grad, 'mp', split_axis=2, concat_axis=1, tiled=True)]
    all_to_all x2 -> x0, starting transfers between devices: 8.5 us -> none  [the longest x1 5 us: local(): lax.all_to_all(local_bias, 'mp', split_axis=1, concat_axis=2, tiled=True)]
  transfers between devices with their start and end apart: 15 -> 0, of which waited for: 11 -> 0; matrix products, arithmetic and copies ran while one was open for 14% -> 0% of each run, Pallas kernels for 0% -> 0%
where the time goes in v1:
time: 225 us; the launch traced here: 222 us
  Pallas kernels  187 us (83%)
  local copies, waits for them, and re-layouts  18.7 us (8%)
  other arithmetic  15.6 us (7%)
    pallas_call x1, Pallas kernels, layer_call(): pl.pallas_call(layer_kernel, out_shape=tuple((jax.ShapeDtypeStruct(s, t)...  173 us
    unnamed x79, local copies, waits for them, and re-layouts  15.4 us
    pallas_call x1, Pallas kernels, pair_call(): pl.pallas_call(pair_kernel, grid=(2, 8), out_shape=jax.ShapeDtypeStruct((...  14 us
    another operation x21, other arithmetic, adamw(): return (jnp.stack([updated, average]), jnp.stack([first, second]))  8.13 us

profile of v1, /device:TPU:0, one launch (start us, length us, event | category | flops | bytes accessed | tf_op | source)
XLA Modules:
  0.0 222.3 jit_solution(12953603425574089997)
XLA Ops:
  0.7 0.8 convert_bitcast_fusion.2
  1.4 0.7 convert.43
  2.3 0.9 convert.44
  3.3 0.1 reshape.407
  3.4 0.7 concatenate.67.ms
  4.1 1.0 copy.203
  5.2 0.8 pad_maximum_fusion.15.am
  6.1 0.8 pad_maximum_fusion.10.es
  6.9 0.1 copy.245
  7.2 0.1 copy.243
  7.5 0.1 copy.247
  7.6 0.1 copy.246
  7.8 0.9 maximum_maximum_fusion
  8.7 0.1 multiply_reduce_fusion
  8.9 0.2 select_reduce_fusion
  9.3 0.6 pad_maximum_fusion.20.sinus
  10.0 0.7 fusion.52.pick
  10.6 0.1 multiply_reduce_fusion.1
  10.9 0.7 reshape.408.mask
  11.6 172.8 %layer.1 = (bf16[512,192]{1,0:T(8,128)(2,1)}, bf16[512,192]{1,0:T(8,128)(2,1)}, bf16[2,1024,256]{2,1,0:T(8,128)(2,1)}, bf16[16,256]{1,0:T(8,128)(2,1)}, f32[96,7...) custom-call(bf16[32,1280]{1,0:T(8,128)(2,1)} %concatenate.67.ms, ...), custom_call_target="tpu_custom_call" | custom-call | tf_op jit(solution)/shard_map/layer/pallas_call | solution.py:1074
  184.4 1.8 copy.235
  186.1 1.8 copy.236
  187.9 14.0 %pair.3 = bf16[2,64,256,256]{3,2,1,0:T(8,128)(2,1)} custom-call(bf16[2,1024,256]{2,1,0:T(8,128)(2,1)} %get-tuple-element.27.ds, bf16[16,256]{1,0:T(8,128)(2,1)} %get-tuple-element.28.pw), custom_call_target="tpu_custom_call" | custom-call | tf_op jit(solution)/shard_map/pair/pallas_call | solution.py:1093
  202.0 1.1 copy-done
  203.1 0.3 fusion.21
  203.3 0.9 pad_maximum_fusion.2
  204.3 0.9 pad_maximum_fusion.3
  205.5 0.2 fusion.40
  205.7 0.8 copy.237
  206.5 0.8 copy.238
  207.3 0.6 fusion.56
  208.0 0.5 copy-done.8
  208.6 0.5 copy-done.2
  209.1 0.5 fusion.9
  209.7 1.9 copy.239
  211.6 0.2 multiply_add_fusion
  211.9 1.9 copy.240
  213.9 0.3 fusion.42
  214.1 0.9 pad_maximum_fusion.6
  215.0 0.9 pad_maximum_fusion.7
  216.1 0.6 fusion.33
  216.8 0.9 copy.241
  217.8 0.3 fusion.35
  218.2 0.9 copy.242
  219.6 0.6 pad_maximum_fusion.18
  220.4 0.6 pad_maximum_fusion.19
  221.1 0.6 pad_maximum_fusion.16
  221.7 0.6 pad_maximum_fusion.17
  (107 shorter events, 3.2 us)
Async XLA Ops:
  0.7 4.5 %copy-start.4 = (f32[96,3,192]{2,0,1:T(8,128)S(1)}, f32[96,3,192]{2,0,1:T(8,128)}, u32[]{:S(2)}) copy-start(f32[96,3,192]{2,0,1:T(8,128)} %param.27) | copy-start | bytes 663556
  2.1 3.8 %copy-start.6 = (f32[768,96]{0,1:T(8,128)S(1)}, f32[768,96]{0,1:T(8,128)}, u32[]{:S(2)}) copy-start(f32[768,96]{0,1:T(8,128)} %param.33) | copy-start | bytes 884740
  3.3 2.7 %copy-start.1 = (f32[96,2,768]{2,1,0:T(2,128)S(1)}, f32[96,2,768]{2,1,0:T(2,128)}, u32[]{:S(2)}) copy-start(f32[96,2,768]{2,1,0:T(2,128)} %param.31) | copy-start | bytes 1769476
  5.1 0.9 copy-start.9
  6.0 0.9 copy-start.16
  6.1 1.2 slice-start
  6.1 1.3 copy-start.17
  6.1 1.5 slice-start.1
  7.1 1.6 copy-start.27
  7.1 1.6 copy-start.24
  7.1 1.8 copy-start.25
  7.1 1.8 copy-start.26
  187.9 14.0 %copy-start.15 = (f32[96,768]{1,0:T(8,128)S(1)}, f32[96,768]{1,0:T(8,128)}, u32[]{:S(2)}) copy-start(f32[96,768]{1,0:T(8,128)} %get-tuple-element.29) | copy-start | bytes 884740
  187.9 14.1 %copy-start.5 = (f32[96,3,192]{2,0,1:T(8,128)S(1)}, f32[96,3,192]{2,0,1:T(8,128)}, u32[]{:S(2)}) copy-start(f32[96,3,192]{2,0,1:T(8,128)} %param.27) | copy-start | bytes 663556
  201.9 1.2 copy-start
  204.2 1.0 copy-start.18
  204.3 1.2 copy-start.10
  205.5 1.9 copy-start.3
  207.3 1.2 copy-start.8
  207.9 1.1 copy-start.2
  211.9 2.0 copy-start.7
  211.9 1.9 copy-start.11
  214.1 1.7 copy-start.14
  215.0 1.0 copy-start.13
  215.0 1.1 copy-start.12
  218.1 1.0 copy-start.23
  218.1 1.1 copy-start.22
  218.1 1.3 copy-start.21
  218.1 2.9 %copy-start.19 = (f32[43,32]{0,1:T(8,128)S(1)}, f32[43,32]{0,1:T(8,128)}, u32[]{:S(2)}) copy-start(f32[43,32]{0,1:T(8,128)} %param.39) | copy-start | bytes 16516
  218.1 2.9 %copy-start.20 = (f32[3,43,32]{1,2,0:T(8,128)S(1)}, f32[3,43,32]{1,2,0:T(8,128)}, u32[]{:S(2)}) copy-start(f32[3,43,32]{1,2,0:T(8,128)} %param.40) | copy-start | bytes 49540

commit v2 on v1

--- a/solution.py
+++ b/solution.py
@@ -492,7 +492,7 @@
 
 def layer_kernel(
     ms, am, es, xp, gp, pair, sinus, pick, mask,
-    out_o, res_o, ds_o, pw_o, am_o, es_o, mod_o, pc_o,
+    out_o, res_o, ds_o, pw_o, at_o, mg_o, ex_o, sh_o, mod_o, pair_o, class_o,
     msg, amg, esg, xg, gg, modu, modg, modf, bpg, pb, bias, n1, sp1, r1,
     kf, vf, qf, pr, mix, att, mid, n2, sp2, r2, fg, act, upg, fp, fl, p2, p2l, p2o, fpo,
     esp, epl, exl, eso, dkv, dkf, dvf, dqf, mgd, l2, rhs2, p1, p1l,
@@ -978,7 +978,9 @@
     for r in (1, 2, 3):
         net.wait(exl.at[r - 1], es_chip + r)
         total = total + exl[r - 1].astype(f32)
-    es_o[...] = total
+    for k in range(2):
+        ex_o[:, k, :] = total[:, 768 * k : 768 * k + 768]
+    sh_o[...] = total[:, 1536:2304]
 
     net.wait(pwl, pw_pair)
     pw_chip = net.sems(4)
@@ -1010,7 +1012,9 @@
     picks = bpg[:, :, 256:384].reshape(64, 128)
     grads = mrg[...].reshape(64, 1152)
     ctf[...] = condition.T
-    mod_o[...] = mm(ctf[pl.ds(pl.multiple_of(d * 32, 32), 32), :], grads, NN, HIGH)
+    mod_sums = mm(ctf[pl.ds(pl.multiple_of(d * 32, 32), 32), :], grads, NN, HIGH)
+    for j in range(6):
+        mod_o[j] = mod_sums[:, 192 * j : 192 * j + 192]
     cond_grad = mm(grads, msg[:, :, 128:1280].reshape(256, 1152).astype(f32), NT, HIGH)
     before_grad = cond_grad * (sig * (1.0 + before * (1.0 - sig)))
     cfull[...] = mm(before_grad, picks, TN, HIGH)
@@ -1029,15 +1033,21 @@
     total = aso[m]
     for t in (1, 3, 2):
         total = total + azl[am_z.wait(t)].astype(f32)
-    am_o[...] = total
+    at_o[0] = total[:, 384:576]
+    at_o[1] = total[:, 0:192]
+    at_o[2] = total[:, 192:384]
+    tall = jnp.concatenate([total[:, 512:768], jnp.zeros((32, 256), f32)], axis=0).T
+    mg_o[...] = tall[64:256, 0:96]
     total = pco[...]
     for t in (1, 3, 2):
         total = total + pcl[pc_line.wait(t)]
-    pc_o[...] = total
+    tall = jnp.concatenate([total[:, 0:128], jnp.zeros((96, 128), f32)], axis=0).T
+    pair_o[...] = tall[0:HEADS, 0:32]
+    class_o[...] = total[:, 128 : 128 + class_o.shape[1]]
     net.drain()
 
 
-def layer_call(*args):
+def layer_call(classes, *args):
     V = pltpu.VMEM
     scratch = [
         V((8, 32, 1280), bf16), V((4, 8, 96, 768), bf16), V((8, 96, 2304), bf16),
@@ -1069,7 +1079,8 @@
     whole = pl.BlockSpec(memory_space=pltpu.VMEM)
     outs = (
         ((512, 192), bf16), ((512, 192), bf16), ((2, 1024, 256), bf16), ((16, 256), bf16),
-        ((96, 768), f32), ((96, 2304), f32), ((32, 1152), f32), ((32, 256), f32),
+        ((3, 96, 192), f32), ((192, 96), f32), ((96, 2, 768), f32), ((96, 768), f32),
+        ((6, 32, 192), f32), ((HEADS, 32), f32), ((32, classes), f32),
     )
     return pl.pallas_call(
         layer_kernel,
@@ -1084,23 +1095,107 @@
     )(*args)
 
 
-def pair_kernel(ds, pw, out):
-    for i in range(8):
-        out[0, i] = mm(ds[0, GROUP * i : GROUP * i + GROUP, :], pw[...], TN).astype(bf16)
-
-
-def pair_call(ds, pw):
+def finish_kernel(*refs):
+    ds, pw, out, res = refs[0:4]
+    groups = [refs[4 + 3 * i : 7 + 3 * i] for i in range(7)]
+    out_t, res_t, pair = refs[25:28]
+    results = [refs[28 + 2 * i : 30 + 2 * i] for i in range(7)]
+    block, sems = refs[42:44]
+    step = pl.program_id(0)
+
+    def put(c, at):
+        rows = pl.ds((at % 2) * 32 + 8 * c, 8)
+        return pltpu.make_async_copy(block.at[c], pair.at[at // 2, rows], sems.at[c])
+
+    def update(index):
+        (master, state, grad), (fresh, kept) = groups[index], results[index]
+        old, slope = master[...], grad[...]
+        first = BETA_ONE * state[0] + (1.0 - BETA_ONE) * slope
+        second = BETA_TWO * state[1] + (1.0 - BETA_TWO) * slope * slope
+        first_hat = first / (1.0 - BETA_ONE**STEP)
+        second_hat = second / (1.0 - BETA_TWO**STEP)
+        new = old - RATES[index] * (first_hat / (jnp.sqrt(second_hat) + ADAM_EPS) + DECAY * old)
+        average = AVERAGE * state[2] + (1.0 - AVERAGE) * new
+        for ref, values in ((fresh, (new, average)), (kept, (first, second))):
+            for i in range(2):
+                if index == 5:
+                    ref[:, i, :] = values[i]
+                else:
+                    ref[i] = values[i]
+
+    def turn(source, target):
+        wide = jnp.concatenate([source[...].astype(f32), jnp.zeros((128, 64), f32)], axis=-1)
+        target[...] = wide.T[0:192, :].astype(bf16)
+
+    for c in range(4):
+
+        @pl.when(step > 0)
+        def _(c=c):
+            put(c, step - 1).wait()
+
+        for i in range(8):
+            at = GROUP * (8 * c + i)
+            block[c, i] = mm(ds[0, at : at + GROUP, :], pw[...], TN).astype(bf16)
+        if c == 0:
+            update(0)
+            update(1)
+            turn(out, out_t)
+        elif c == 1:
+            update(2)
+        elif c == 2:
+            update(3)
+            turn(res, res_t)
+        else:
+            for index in (4, 5, 6):
+                update(index)
+        put(c, step).start()
+
+    @pl.when(step == 3)
+    def _():
+        for c in range(4):
+            put(c, step).wait()
+
+
+def finish_call(ds, pw, out, res, *groups):
+    def rows(shape, axis=-2):
+        at = len(shape) + axis
+        block = (*shape[:at], shape[at] // 4, *shape[at + 1 :])
+        return pl.BlockSpec(block, lambda i: (0,) * at + (i,) + (0,) * (-1 - axis))
+
+    def whole(shape):
+        return pl.BlockSpec(tuple(shape), lambda i: (0,) * len(shape))
+
+    in_specs = [
+        pl.BlockSpec((1, 512, 256), lambda i: (i // 2, i % 2, 0)), whole((16, 256)),
+        rows((512, 192)), rows((512, 192)),
+    ]
+    turned = pl.BlockSpec((192, 128), lambda i: (0, i))
+    out_specs = [turned, turned, pl.BlockSpec(memory_space=pl.ANY)]
+    outs = [
+        jax.ShapeDtypeStruct((192, 512), bf16), jax.ShapeDtypeStruct((192, 512), bf16),
+        jax.ShapeDtypeStruct((2, 64, 256, 256), bf16),
+    ]
+    for index in range(7):
+        master, state, grad = groups[3 * index : 3 * index + 3]
+        make = rows if index < 5 else whole
+        if index == 2:
+            make = lambda shape: rows(shape, -3)
+        in_specs += [make(master.shape), make(state.shape), make(grad.shape)]
+        shape = (2, *master.shape)
+        if index == 5:
+            shape = (master.shape[0], 2, master.shape[1])
+        out_specs += [make(shape)] * 2
+        outs += [jax.ShapeDtypeStruct(shape, f32)] * 2
     return pl.pallas_call(
-        pair_kernel,
-        grid=(2, 8),
-        out_shape=jax.ShapeDtypeStruct((2, 64, 256, 256), bf16),
-        in_specs=[
-            pl.BlockSpec((1, 128, 256), lambda w, i: (w, i, 0)),
-            pl.BlockSpec((16, 256), lambda w, i: (0, 0)),
-        ],
-        out_specs=pl.BlockSpec((1, 8, 256, 256), lambda w, i: (w, i, 0, 0)),
-        name="pair",
-    )(ds, pw)
+        finish_kernel,
+        grid=(4,),
+        out_shape=tuple(outs),
+        in_specs=in_specs,
+        out_specs=tuple(out_specs),
+        scratch_shapes=[pltpu.VMEM((4, 8, 256, 256), bf16), pltpu.SemaphoreType.DMA((4,))],
+        compiler_params=pltpu.CompilerParams(vmem_limit_bytes=67043328),
+        name="finish",
+    )(ds, pw, out, res, *groups)
 
 
 def fast_local(
@@ -1146,19 +1241,20 @@
     seen = jnp.where(unit_slot == mine, 0.0, MASKED)
     mask = jnp.broadcast_to(seen[:, :, None], (2, 4, UNIT)).reshape(2, 256)
 
-    out, res, ds, pw, am_g, es_g, mod_g, pc_g = layer_call(
-        ms, am, es, packed(residues), packed(out_grad), pair_input, sinus, pick, mask
-    )
-    pair_grad = pair_call(ds, pw)
-    grads = (
-        jnp.stack([am_g[:, 384:576], am_g[:, 0:192], am_g[:, 192:384]], axis=1),
-        am_g[:, 576:768].T,
-        jnp.stack([es_g[:, 0:768], es_g[:, 768:1536]], axis=1),
-        es_g[:, 1536:2304].T,
-        mod_g.reshape(32, 6, 192),
-        pc_g[:, 0:HEADS],
-        pc_g[:, 128 : 128 + classes].T,
-    )
+    out, res, ds, pw, *grads = layer_call(
+        classes, ms, am, es, packed(residues), packed(out_grad), pair_input, sinus, pick, mask
+    )
+
+    def thirds(v):
+        return jnp.swapaxes(v, -3, -2).reshape(*v.shape[:-3], -1, v.shape[-1])
+
+    def turned(v):
+        return jnp.swapaxes(v, -2, -1)
+
+    def same(v):
+        return v
+
+    views = (thirds, same, same, turned, thirds, turned, turned)
     masters = (
         attend_weight, merge_weight, expand_weight, shrink_weight, modulate_weight, pair_weight,
         class_weight,
@@ -1167,10 +1263,21 @@
         attend_state, merge_state, expand_state, shrink_state, modulate_state, pair_state,
         class_state,
     )
-    results = []
-    for master, state, grad, rate in zip(masters, states, grads, RATES):
-        results.extend(adamw(master, state, grad, rate))
-    return (out, res, pair_grad, *results)
+    groups = []
+    for view, master, state, grad in zip(views, masters, states, grads):
+        master = view(master)
+        groups += [master, view(state), grad.reshape(master.shape)]
+    out, res, pair_grad, *results = finish_call(ds, pw, out, res, *groups)
+
+    def back(index, v):
+        if index in (0, 4):
+            count = masters[index].shape[1]
+            return jnp.swapaxes(v.reshape(2, count, -1, v.shape[-1]), 1, 2)
+        if index == 5:
+            return jnp.transpose(v, (1, 2, 0))
+        return v if index in (1, 2) else turned(v)
+
+    return (out.T, res.T, pair_grad, *(back(i // 2, v) for i, v in enumerate(results)))
 
 
 def solution(mesh):

time: 225 us -> 204 us (0.907)
  local copies, waits for them, and re-layouts: 18.7 us -> 5.32 us
  other arithmetic: 15.6 us -> 8.93 us
    unnamed x79 -> x14, local copies, waits for them, and re-layouts: 15.4 us -> 1.72 us
    another operation x24 -> x5, other arithmetic: 9.79 us -> 2.4 us  [the longest x21 8.13 us: adamw(): return (jnp.stack([updated, average]), jnp.stack([first, second]))]
where the time goes in v2:
time: 204 us; the launch traced here: 202 us
  Pallas kernels  187 us (92%)
  other arithmetic  8.93 us (4%)
  local copies, waits for them, and re-layouts  5.32 us (3%)
    pallas_call x1, Pallas kernels, layer_call(): pl.pallas_call(layer_kernel, out_shape=tuple((jax.ShapeDtypeStruct(s, t)...  173 us
    pallas_call x1, Pallas kernels, finish_call(): pl.pallas_call(finish_kernel, grid=(4,), out_shape=tuple(outs), in_specs=...  14.2 us

profile of v2, /device:TPU:0, one launch (start us, length us, event | category | flops | bytes accessed | tf_op | source)
XLA Modules:
  0.0 202.5 jit_solution(3322824760194699427)
XLA Ops:
  0.7 0.0 slice-start.1
  0.7 0.0 slice-start
  0.7 0.8 compare_convert_fusion.1
  1.5 0.8 multiply_reduce_fusion
  2.3 0.1 multiply_reduce_fusion.1
  2.4 0.1 compare_select_fusion
  2.5 0.9 select_reduce_fusion
  3.4 0.1 eq.74
  3.5 0.1 mul.73
  3.6 0.7 fusion.pick
  4.3 0.1 broadcast_in_dim.10
  4.3 0.7 reshape.144.mask
  5.0 0.7 convert.41
  5.7 0.1 copy.68
  5.8 0.1 multiply_sine_fusion
  5.9 0.6 pad_maximum_fusion.2.sinus
  6.5 0.7 bitcast_convert_fusion.1
  7.3 1.0 copy.70
  8.2 0.0 copy-start.1
  8.3 0.8 fusion.2
  9.1 0.1 copy.79
  9.2 0.1 copy.80
  9.3 0.8 fusion.1
  10.1 0.1 copy.82
  10.2 0.1 copy.83
  10.3 0.9 convert.42
  11.3 0.1 copy.69
  11.4 0.0 copy-start.2
  11.4 0.1 reshape.143
  11.5 0.7 concatenate.27.ms
  12.2 0.0 copy-start
  12.2 0.0 slice-done
  12.2 0.1 copy.78
  12.4 0.0 slice-done.1
  12.4 0.1 copy.81
  12.5 0.9 maximum_maximum_fusion
  13.4 0.0 copy-done.1
  13.4 0.8 pad_maximum_fusion.1.am
  14.2 0.0 copy-done.2
  14.2 0.0 copy-done
  14.3 0.8 pad_maximum_fusion.es
  15.1 173.0 %layer.1 = (bf16[512,192]{1,0:T(8,128)(2,1)}, bf16[512,192]{1,0:T(8,128)(2,1)}, bf16[2,1024,256]{2,1,0:T(8,128)(2,1)}, bf16[16,256]{1,0:T(8,128)(2,1)}, f32[3,96...) custom-call(bf16[32,1280]{1,0:T(8,128)(2,1)} %concatenate.27.ms, ...), custom_call_target="tpu_custom_call" | custom-call | tf_op jit(solution)/shard_map/layer/pallas_call | solution.py:1085
  188.1 14.2 %finish.1 = (bf16[192,512]{1,0:T(8,128)(2,1)}, bf16[192,512]{1,0:T(8,128)(2,1)}, bf16[2,64,256,256]{3,2,1,0:T(8,128)(2,1)}, f32[2,288,192]{2,1,0:T(8,128)}, f32[...) custom-call(bf16[2,1024,256]{2,1,0:T(8,128)(2,1)} %get-tuple-element, ...), custom_call_target="tpu_custom_call" | custom-call | tf_op jit(solution)/shard_map/finish/pallas_call | solution.py:1189
  (10 shorter events, 0.1 us)
Async XLA Ops:
  0.7 11.7 %slice-start.1 = ((bf16[512,192]{0,1:T(8,128)(2,1)}), bf16[512,128]{0,1:T(8,128)(2,1)S(1)}, s32[]{:S(2)}) async-start(bf16[512,192]{0,1:T(8,128)(2,1)} %param.23), calls=%async_computation.1 | async-start | bytes 262144 | tf_op jit(solution)/shard_map/slice | solution.py:1226
  0.7 11.6 %slice-start = ((bf16[512,192]{0,1:T(8,128)(2,1)}), bf16[512,128]{0,1:T(8,128)(2,1)S(1)}, s32[]{:S(2)}) async-start(bf16[512,192]{0,1:T(8,128)(2,1)} %param.21), calls=%async_computation | async-start | bytes 262144 | tf_op jit(solution)/shard_map/slice | solution.py:1226
  8.2 5.1 %copy-start.1 = (f32[96,3,192]{2,0,1:T(8,128)S(1)}, f32[96,3,192]{2,0,1:T(8,128)}, u32[]{:S(2)}) copy-start(f32[96,3,192]{2,0,1:T(8,128)} %param.27) | copy-start | bytes 663556
  11.4 2.8 %copy-start.2 = (f32[768,96]{0,1:T(8,128)S(1)}, f32[768,96]{0,1:T(8,128)}, u32[]{:S(2)}) copy-start(f32[768,96]{0,1:T(8,128)} %param.33) | copy-start | bytes 884740
  12.2 2.0 copy-start

commit v3 on v2

--- a/solution.py
+++ b/solution.py
@@ -466,7 +466,7 @@
         net = self.net
         slot = self.slot(net.peer(r))
         net.wait(slot, self.base + r)
-        return net.send(slot, slot, self.base + 3 + r, (net.partner, net.m))
+        return [net.send(slot, slot, self.base + 3 + r, (net.partner, net.m))]
 
     def finish(self):
         net = self.net
@@ -518,7 +518,8 @@
     for step in range(slots):
         pair_copy(step).start()
 
-    ms_all = Spread(net, lambda i: msg.at[i])
+    cp_all = Spread(net, lambda i: msg.at[i, :, 0:128])
+    ms_all = Spread(net, lambda i: msg.at[i, :, 128:1280])
     am_line = Zline(net, lambda s: amg.at[s, d])
     am_all = [Spread(net, lambda i, t=t: amg.at[net.z(t), i]) for t in range(4)]
     x_line = Zline(net, lambda s: xg.at[s])
@@ -527,20 +528,19 @@
     bp_all = Spread(net, lambda i: bpg.at[i])
     es_all = Spread(net, lambda i: esg.at[i])
 
-    ms_all.start(ms)
-    for t in (1, 2, 3):
+    cp_all.start(ms.at[:, 0:128])
+    for t in (1, 3, 2):
         am_line.send(t, am)
+    ms_all.start(ms.at[:, 128:1280])
     am_all[0].start(am)
-    for t in (1, 2, 3):
-        x_line.send(t, xp)
     msg[d] = ms[...]
     amg[m, d] = am[...]
     esg[d] = es[...]
     xg[m] = xp[...]
     gg[m] = gp[...]
     for r in (1, 2, 3):
-        ms_all.forward(r)
-    ms_all.finish()
+        cp_all.forward(r)
+    cp_all.finish()
 
     slab = msg[:, :, 0:128].reshape(256, 128)
     select = (
@@ -550,10 +550,6 @@
     pw_o[...] = mm(jnp.where(select, 1.0, 0.0).astype(bf16), slab, NT).astype(bf16)
     before = sinus[...] + mm(pick[...], slab, NT)
     condition = (before * jax.nn.sigmoid(before)).astype(bf16)
-    modu[...] = mm(condition, msg[:, :, 128:1280].reshape(256, 1152))
-    for t in (1, 2, 3):
-        mod_line.send(t, modu)
-    modg[m] = modu[...]
     bpg[d] = jnp.concatenate([before, pick[...].astype(f32)], axis=-1)
 
     def bias_chunk(step):
@@ -569,26 +565,46 @@
         lax.fori_loop(0, PAIRS, one, 0, unroll=4)
         pair_copy(step + slots).start()
 
-    for step in range(4):
+    bias_chunk(0)
+    bias_chunk(1)
+    for r in (1, 2, 3):
+        ms_all.forward(r)
+    bias_chunk(2)
+    am_line.wait(1)
+    am_all[1].start()
+    bias_chunk(3)
+    ms_all.finish()
+    modu[...] = mm(condition, msg[:, :, 128:1280].reshape(256, 1152))
+    modg[m] = modu[...]
+    am_line.wait(3)
+    am_all[3].start()
+    bias_chunk(4)
+    for r in (1, 2):
+        am_all[0].forward(r)
+    bias_chunk(5)
+    am_line.wait(2)
+    am_all[2].start()
+    for t in (1, 2, 3):
+        x_line.send(t, xp)
+    for t in (1, 2, 3):
+        mod_line.send(t, modu)
+    bias_chunk(6)
+    am_all[0].forward(3)
+    bias_chunk(7)
+    for r in (1, 2):
+        am_all[1].forward(r)
+    for step in (8, 9, 10):
         bias_chunk(step)
-    for t in (1, 3, 2):
-        am_line.wait(t)
-        am_all[t].start()
-        first = {1: 4, 3: 6, 2: 8}[t]
-        bias_chunk(first)
-        bias_chunk(first + 1)
-    for r in (1, 2, 3):
-        am_all[0].forward(r)
-    es_all.start(es)
-    for t in (1, 2, 3):
-        g_line.send(t, gp)
-    bp_all.start()
-    bias_chunk(10)
-    bias_chunk(11)
-    for r in (1, 2, 3):
-        am_all[1].forward(r)
-    for step in range(12, 16):
+    am_all[1].forward(3)
+    for r in (1, 2):
+        am_all[3].forward(r)
+    for step in (11, 12, 13):
         bias_chunk(step)
+    am_all[3].forward(3)
+    for r in (1, 2):
+        am_all[2].forward(r)
+    bias_chunk(14)
+    bias_chunk(15)
 
     for t in (1, 2, 3):
         mod_line.wait(t)
@@ -625,9 +641,11 @@
 
         lax.fori_loop(0, 4, first_norm, 0)
 
-    for t in (3, 2):
-        for r in (1, 2, 3):
-            am_all[t].forward(r)
+    am_all[2].forward(3)
+    es_all.start(es)
+    for t in (1, 2, 3):
+        g_line.send(t, gp)
+    bp_all.start()
     for t in (0, 1, 3, 2):
         am_all[t].finish()
 
@@ -663,34 +681,34 @@
         mix[mine, :] = merge_heads(mm(chance.astype(bf16), vf[keys, :])).astype(bf16)
         return carry
 
-    lax.fori_loop(0, 8, attend, 0)
-    es_sent = [es_all.forward(r) for r in (1, 2, 3)]
-
-    mixed = mix[...]
-    blank = jnp.zeros((128, 192), bf16)
-    attended = mm(
-        jnp.concatenate([blank, mixed[:, 0:192]], axis=-1), weight(0, 384, 768), NT
-    )
-    for s in range(1, 4):
-        part = jnp.concatenate([blank, mixed[:, 192 * s : 192 * s + 192]], axis=-1)
-        attended = attended + mm(part, weight(s, 384, 768), NT)
-    att[...] = attended
-
     def mod_row(j, w):
         return modf[j, pl.ds(w * 4 + m, 1), :]
 
+    blank = jnp.zeros((128, 192), bf16)
+    r2_lines = []
+    es_sent = []
     for w in range(2):
         half = slice(w * UNIT, w * UNIT + UNIT)
-        middle = unpack(xg, w, m) + mod_row(2, w) * att[half, :]
+        lax.fori_loop(4 * w, 4 * w + 4, attend, 0)
+        mixed = mix[half, :]
+        attended = 0.0
+        for s in range(4):
+            part = jnp.concatenate([blank[:UNIT], mixed[:, 192 * s : 192 * s + 192]], axis=-1)
+            attended = attended + mm(part, weight(s, 384, 768), NT)
+        att[half, :] = attended
+        middle = unpack(xg, w, m) + mod_row(2, w) * attended
         mid[half, :] = middle
         normed, spread = norm(middle)
         n2[half, :] = normed
         sp2[half, :] = jnp.broadcast_to(spread, (UNIT, 128))
         r2[m, half, :] = (normed * (1.0 + mod_row(4, w)) + mod_row(3, w)).astype(bf16)
-
-    r2_line = Zline(net, lambda s: r2.at[s])
-    for t in (1, 3, 2):
-        r2_line.send(t, r2.at[m])
+        line = Zline(net, lambda s, half=half: r2.at[s, half])
+        r2_lines.append(line)
+        for t in (1, 3, 2):
+            line.send(t, r2.at[m, half])
+        for r in ((1, 2), (3,))[w]:
+            es_sent += es_all.forward(r)
+
     for t in (1, 2, 3):
         g_line.wait(t)
     for s in range(4):
@@ -725,13 +743,12 @@
     p2o[...] = partial
     fpo[...] = fed
     for t in (1, 3, 2):
-        source = r2_line.wait(t)
+        for line in r2_lines:
+            source = line.wait(t)
         partial, fed = feed(source)
         p2[source] = partial.astype(bf16)
         p2_line.send(t, p2.at[source])
         fp[source] = fed.astype(bf16)
-    for t in (1, 3, 2):
-        f_line.send(t, fp.at[net.z(t)])
 
     def put_es(left, right, at):
         for h in range(2):
@@ -750,6 +767,8 @@
 
     for t in (1, 3, 2):
         p2_line.wait(t)
+    for t in (1, 3, 2):
+        f_line.send(t, fp.at[net.z(t)])
 
     def norm_back(upstream, normed, spread, scale):
         inner = upstream * (1.0 + scale)
@@ -961,6 +980,22 @@
     mr_all = Spread(net, lambda i: mrg.at[i])
     mr_all.start()
 
+    am_z = Zline(net, lambda s: azl.at[s])
+
+    def am_arrive(t):
+        s = net.z(t)
+        total = aso[s]
+        for r in (1, 2, 3):
+            net.wait(axl.at[s, r - 1], am_chip + 4 * t + r)
+            total = total + axl[s, r - 1].astype(f32)
+        if t:
+            azs[s] = total.astype(bf16)
+            am_z.send(t, azs.at[s])
+        else:
+            aso[s] = total
+
+    am_arrive(1)
+
     for t in (1, 3, 2):
         p1_line.wait(t)
     r_line = Zline(net, lambda s: rpl.at[s])
@@ -974,6 +1009,9 @@
         done.append(p2o[half, :] + back)
     pack(r_line, jnp.concatenate(done, axis=0), rps)
 
+    am_arrive(3)
+    am_arrive(2)
+
     total = eso[...]
     for r in (1, 2, 3):
         net.wait(exl.at[r - 1], es_chip + r)
@@ -989,21 +1027,9 @@
         net.send(pwx.at[r], pwy.at[r], pw_chip + r, (net.peer(r), m))
     pair_sum = pws[net.core, net.chip] + pwl[net.chip]
 
-    am_z = Zline(net, lambda s: azl.at[s])
-    for t in (1, 3, 2, 0):
-        s = net.z(t)
-        total = aso[s]
-        for r in (1, 2, 3):
-            net.wait(axl.at[s, r - 1], am_chip + 4 * t + r)
-            total = total + axl[s, r - 1].astype(f32)
-        if t:
-            azs[s] = total.astype(bf16)
-            am_z.send(t, azs.at[s])
-        else:
-            aso[s] = total
-        if t == 1:
-            for r in (1, 2, 3):
-                mr_all.forward(r)
+    for r in (1, 2, 3):
+        mr_all.forward(r)
+    am_arrive(0)
 
     mr_all.finish()
     before = bpg[:, :, 0:256].reshape(64, 256)

time: 204 us -> 193 us (0.946)
  Pallas kernels: 187 us -> 177 us
    pallas_call x1, Pallas kernels: 173 us -> 163 us  [layer_call(): pl.pallas_call(layer_kernel, out_shape=tuple((jax.ShapeDtypeStruct(s, t)...]
where the time goes in v3:
time: 193 us; the launch traced here: 192 us
  Pallas kernels  177 us (92%)
  other arithmetic  8.93 us (5%)
  local copies, waits for them, and re-layouts  5.32 us (3%)
    pallas_call x1, Pallas kernels, layer_call(): pl.pallas_call(layer_kernel, out_shape=tuple((jax.ShapeDtypeStruct(s, t)...  163 us
    pallas_call x1, Pallas kernels, finish_call(): pl.pallas_call(finish_kernel, grid=(4,), out_shape=tuple(outs), in_specs=...  14.2 us

profile of v3, /device:TPU:0, one launch (start us, length us, event | category | flops | bytes accessed | tf_op | source)
XLA Modules:
  0.0 192.5 jit_solution(102972975211067393)
XLA Ops:
  0.7 0.0 slice-start.1
  0.7 0.0 slice-start
  0.7 0.8 compare_convert_fusion.1
  1.5 0.8 multiply_reduce_fusion
  2.3 0.1 multiply_reduce_fusion.1
  2.4 0.1 compare_select_fusion
  2.5 0.9 select_reduce_fusion
  3.4 0.1 eq.74
  3.5 0.1 mul.73
  3.6 0.7 fusion.pick
  4.3 0.1 broadcast_in_dim.10
  4.3 0.7 reshape.144.mask
  5.0 0.7 convert.41
  5.7 0.1 copy.68
  5.8 0.1 multiply_sine_fusion
  5.9 0.6 pad_maximum_fusion.2.sinus
  6.5 0.7 bitcast_convert_fusion.1
  7.3 1.0 copy.70
  8.2 0.0 copy-start.1
  8.3 0.8 fusion.2
  9.1 0.1 copy.79
  9.2 0.1 copy.80
  9.3 0.8 fusion.1
  10.1 0.1 copy.82
  10.2 0.1 copy.83
  10.3 0.9 convert.42
  11.3 0.1 copy.69
  11.4 0.0 copy-start.2
  11.4 0.1 reshape.143
  11.5 0.7 concatenate.27.ms
  12.2 0.0 copy-start
  12.2 0.0 slice-done
  12.2 0.1 copy.78
  12.4 0.0 slice-done.1
  12.4 0.1 copy.81
  12.5 0.9 maximum_maximum_fusion
  13.4 0.0 copy-done.1
  13.4 0.8 pad_maximum_fusion.1.am
  14.2 0.0 copy-done.2
  14.2 0.0 copy-done
  14.3 0.8 pad_maximum_fusion.es
  15.1 163.0 %layer.1 = (bf16[512,192]{1,0:T(8,128)(2,1)}, bf16[512,192]{1,0:T(8,128)(2,1)}, bf16[2,1024,256]{2,1,0:T(8,128)(2,1)}, bf16[16,256]{1,0:T(8,128)(2,1)}, f32[3,96...) custom-call(bf16[32,1280]{1,0:T(8,128)(2,1)} %concatenate.27.ms, ...), custom_call_target="tpu_custom_call" | custom-call | tf_op jit(solution)/shard_map/layer/pallas_call | solution.py:1111
  178.1 14.2 %finish.1 = (bf16[192,512]{1,0:T(8,128)(2,1)}, bf16[192,512]{1,0:T(8,128)(2,1)}, bf16[2,64,256,256]{3,2,1,0:T(8,128)(2,1)}, f32[2,288,192]{2,1,0:T(8,128)}, f32[...) custom-call(bf16[2,1024,256]{2,1,0:T(8,128)(2,1)} %get-tuple-element, ...), custom_call_target="tpu_custom_call" | custom-call | tf_op jit(solution)/shard_map/finish/pallas_call | solution.py:1215
  (10 shorter events, 0.1 us)
Async XLA Ops:
  0.7 11.7 %slice-start.1 = ((bf16[512,192]{0,1:T(8,128)(2,1)}), bf16[512,128]{0,1:T(8,128)(2,1)S(1)}, s32[]{:S(2)}) async-start(bf16[512,192]{0,1:T(8,128)(2,1)} %param.23), calls=%async_computation.1 | async-start | bytes 262144 | tf_op jit(solution)/shard_map/slice | solution.py:1252
  0.7 11.6 %slice-start = ((bf16[512,192]{0,1:T(8,128)(2,1)}), bf16[512,128]{0,1:T(8,128)(2,1)S(1)}, s32[]{:S(2)}) async-start(bf16[512,192]{0,1:T(8,128)(2,1)} %param.21), calls=%async_computation | async-start | bytes 262144 | tf_op jit(solution)/shard_map/slice | solution.py:1252
  8.2 5.1 %copy-start.1 = (f32[96,3,192]{2,0,1:T(8,128)S(1)}, f32[96,3,192]{2,0,1:T(8,128)}, u32[]{:S(2)}) copy-start(f32[96,3,192]{2,0,1:T(8,128)} %param.27) | copy-start | bytes 663556
  11.4 2.8 %copy-start.2 = (f32[768,96]{0,1:T(8,128)S(1)}, f32[768,96]{0,1:T(8,128)}, u32[]{:S(2)}) copy-start(f32[768,96]{0,1:T(8,128)} %param.33) | copy-start | bytes 884740
  12.2 2.0 %copy-start = (f32[96,2,768]{2,1,0:T(2,128)S(1)}, f32[96,2,768]{2,1,0:T(2,128)}, u32[]{:S(2)}) copy-start(f32[96,2,768]{2,1,0:T(2,128)} %refs_10_.1) | copy-start | bytes 1769476

commit v4 on v3

--- a/solution.py
+++ b/solution.py
@@ -458,9 +458,8 @@
         net = self.net
         own = self.slot(net.d)
         src = own if src is None else src
-        for r in (1, 2, 3):
-            net.send(src, own, self.base + r, (net.peer(r), net.m))
-        net.send(src, own, self.base, (net.partner, net.m))
+        made = [net.send(src, own, self.base + r, (net.peer(r), net.m)) for r in (1, 2, 3)]
+        return made + [net.send(src, own, self.base, (net.partner, net.m))]
 
     def forward(self, r):
         net = self.net
@@ -491,18 +490,17 @@
 
 
 def layer_kernel(
-    ms, am, es, xp, gp, pair, sinus, pick, mask,
+    aw, mw, ew, sw, ow, pwt, cwt, xt, gt, pair, waves, layout, bins, kinds,
     out_o, res_o, ds_o, pw_o, at_o, mg_o, ex_o, sh_o, mod_o, pair_o, class_o,
-    msg, amg, esg, xg, gg, modu, modg, modf, bpg, pb, bias, n1, sp1, r1,
+    msg, amg, esg, xg, gg, modu, modg, modf, bpg, pb, n1, sp1, r1,
     kf, vf, qf, pr, mix, att, mid, n2, sp2, r2, fg, act, upg, fp, fl, p2, p2l, p2o, fpo,
-    esp, epl, exl, eso, dkv, dkf, dvf, dqf, mgd, l2, rhs2, p1, p1l,
+    esp, epl, exl, dkv, dkf, dvf, dqf, mgd, l2, rhs2, p1, p1l,
     amp, axl, aso, azs, azl, mps, mpl, mrg, pws, pwl, pwx, pwy, pco, pcl,
     ops, opl, rps, rpl, ctf, cfull,
-    send_sems, recv_sems, pair_sems,
+    mask, send_sems, recv_sems, pair_sems,
 ):
     net = Net(send_sems, recv_sems)
     d, m = net.d, net.m
-    net.barrier()
 
     chunks = 16
     slots = pb.shape[0]
@@ -517,6 +515,48 @@
 
     for step in range(slots):
         pair_copy(step).start()
+
+    dkf[0:256, 0:128] = jnp.zeros((256, 128), f32)
+    dkf[0:192, 0:96] = mw[...]
+    tall = dkf[0:256, 0:128].T
+    amg[m, d] = jnp.concatenate([aw[1], aw[2], aw[0], tall[0:96, 0:192]], axis=-1).astype(bf16)
+    cfull[...] = jnp.zeros_like(cfull)
+    cfull[0:HEADS, 0:32] = pwt[...]
+    cfull[128:160, 0 : cwt.shape[1]] = cwt[...]
+    narrow = [cfull[128:160, 0:64], cfull[0:128, :].T[0:32, 0:64]]
+    msg[d] = jnp.concatenate(narrow + [ow[j] for j in range(6)], axis=-1).astype(bf16)
+    net.barrier()
+
+    row8 = lax.broadcasted_iota(jnp.int32, (8, 128), 0)
+    lane8 = lax.broadcasted_iota(jnp.int32, (8, 128), 1)
+    bin8 = jnp.zeros((8, 128), jnp.int32)
+    kind8 = jnp.zeros((8, 128), jnp.int32)
+    mask_row = lax.broadcasted_iota(jnp.int32, (8, 256), 0)
+    mask_unit = lax.broadcasted_iota(jnp.int32, (8, 256), 1) // UNIT
+    seen = jnp.zeros((8, 256), f32)
+    for w in range(2):
+        at = layout[w]
+        held = []
+        for u in range(4):
+            slot = jnp.int32(0)
+            for k in range(5):
+                slot = jnp.where(at == k, jnp.int32(int(PATTERNS[k, u])), slot)
+            held.append(slot)
+        mine = jnp.int32(0)
+        for u in range(4):
+            mine = jnp.where(m == u, held[u], mine)
+        for u in range(4):
+            time, kind = jnp.int32(0), jnp.int32(0)
+            for i in range(4):
+                time = jnp.where(held[u] == i, bins[w, i], time)
+                kind = jnp.where(held[u] == i, kinds[w, i], kind)
+            bin8 = jnp.where(row8 == 4 * w + u, time, bin8)
+            kind8 = jnp.where(row8 == 4 * w + u, kind, kind8)
+            value = jnp.where(held[u] == mine, 0.0, MASKED)
+            seen = jnp.where((mask_row == w) & (mask_unit == u), value, seen)
+    mask[...] = seen
+    pick = jnp.where(lane8 == kind8, 1.0, 0.0).astype(bf16)
+    sinus = mm(jnp.where(lane8 == bin8, 1.0, 0.0), waves[...], NN, HIGH)
 
     cp_all = Spread(net, lambda i: msg.at[i, :, 0:128])
     ms_all = Spread(net, lambda i: msg.at[i, :, 128:1280])
@@ -528,16 +568,21 @@
     bp_all = Spread(net, lambda i: bpg.at[i])
     es_all = Spread(net, lambda i: esg.at[i])
 
-    cp_all.start(ms.at[:, 0:128])
+    cp_all.start()
     for t in (1, 3, 2):
-        am_line.send(t, am)
-    ms_all.start(ms.at[:, 128:1280])
-    am_all[0].start(am)
-    msg[d] = ms[...]
-    amg[m, d] = am[...]
-    esg[d] = es[...]
-    xg[m] = xp[...]
-    gg[m] = gp[...]
+        am_line.send(t, amg.at[m, d])
+    ms_all.start()
+    am_all[0].start()
+    esg[d] = jnp.concatenate([ew[:, 0, :], ew[:, 1, :], sw[...]], axis=-1).astype(bf16)
+
+    def pack_rows(source, ref):
+        wide = jnp.concatenate([source[...], jnp.zeros((64, 512), bf16)], axis=0).T
+        ref[m, 0:512, :] = wide[:, 0:128]
+        low = wide[:, 128:192]
+        ref[m, 512:768, :] = jnp.concatenate([low[0:256], low[256:512]], axis=-1)
+
+    pack_rows(xt, xg)
+    pack_rows(gt, gg)
     for r in (1, 2, 3):
         cp_all.forward(r)
     cp_all.finish()
@@ -548,9 +593,9 @@
         == lax.broadcasted_iota(jnp.int32, (GROUP, 128), 0) + 64
     ) & (lax.broadcasted_iota(jnp.int32, (GROUP, 128), 0) < HEADS)
     pw_o[...] = mm(jnp.where(select, 1.0, 0.0).astype(bf16), slab, NT).astype(bf16)
-    before = sinus[...] + mm(pick[...], slab, NT)
+    before = sinus + mm(pick, slab, NT)
     condition = (before * jax.nn.sigmoid(before)).astype(bf16)
-    bpg[d] = jnp.concatenate([before, pick[...].astype(f32)], axis=-1)
+    bpg[d] = jnp.concatenate([before, pick.astype(f32)], axis=-1)
 
     def bias_chunk(step):
         slot = step % slots
@@ -559,7 +604,7 @@
         def one(i, carry):
             part = mm(pw_o[...], pb[slot, i], NT)
             at = pl.multiple_of((step % 8) * PAIRS * GROUP + i * GROUP, GROUP)
-            bias[step // 8, pl.ds(at, GROUP), :] = part.astype(bf16)
+            ds_o[step // 8, pl.ds(at, GROUP), :] = part.astype(bf16)
             return carry
 
         lax.fori_loop(0, PAIRS, one, 0, unroll=4)
@@ -585,7 +630,7 @@
     am_line.wait(2)
     am_all[2].start()
     for t in (1, 2, 3):
-        x_line.send(t, xp)
+        x_line.send(t, xg.at[m])
     for t in (1, 2, 3):
         mod_line.send(t, modu)
     bias_chunk(6)
@@ -642,9 +687,9 @@
         lax.fori_loop(0, 4, first_norm, 0)
 
     am_all[2].forward(3)
-    es_all.start(es)
+    es_sent = es_all.start()
     for t in (1, 2, 3):
-        g_line.send(t, gp)
+        g_line.send(t, gg.at[m])
     bp_all.start()
     for t in (0, 1, 3, 2):
         am_all[t].finish()
@@ -673,7 +718,7 @@
         keys = pl.ds(pl.multiple_of(w * 256, 256), 256)
         wide = pl.ds(pl.multiple_of((c % 4) * CHUNK * GROUP, CHUNK * GROUP), CHUNK * GROUP)
         scores = mm(spread_heads(qf[mine, :]), kf[keys, :], NT) * factor
-        scores = scores + bias[w, wide, :].astype(f32) + mask[pl.ds(w, 1), :]
+        scores = scores + ds_o[w, wide, :].astype(f32) + mask[pl.ds(w, 1), :]
         peak = jnp.max(scores, axis=-1, keepdims=True)
         expo = jnp.exp(scores - peak)
         chance = expo / jnp.sum(expo, axis=-1, keepdims=True)
@@ -686,7 +731,6 @@
 
     blank = jnp.zeros((128, 192), bf16)
     r2_lines = []
-    es_sent = []
     for w in range(2):
         half = slice(w * UNIT, w * UNIT + UNIT)
         lax.fori_loop(4 * w, 4 * w + 4, attend, 0)
@@ -801,15 +845,10 @@
 
     net.wait(epl, es_pair)
     es_chip = net.sems(4)
-    for r in (1, 2, 3, 0):
+    for r in (1, 2, 3):
         total = esp[net.core, net.chips[r]].astype(f32) + epl[net.chips[r]].astype(f32)
-        if r == 0:
-            eso[...] = total
-        else:
-            esp[net.core, net.chips[r]] = total.astype(bf16)
-            net.send(
-                esp.at[net.core, net.chips[r]], exl.at[r - 1], es_chip + r, (net.peer(r), m)
-            )
+        esp[net.core, net.chips[r]] = total.astype(bf16)
+        net.send(esp.at[net.core, net.chips[r]], exl.at[r - 1], es_chip + r, (net.peer(r), m))
 
     dkf[...] = jnp.zeros_like(dkf)
     dvf[...] = jnp.zeros_like(dvf)
@@ -939,24 +978,20 @@
 
     pairwise = jnp.zeros((GROUP, 256), f32)
     am_chip = net.sems(16)
+
+    def am_total(t, r):
+        base, cols = 4 * (t // 3), slice(768 * (t % 3), 768 * (t % 3) + 768)
+        total = amp[net.z(t), net.core, net.chips[r]].astype(f32)
+        return total + esg[base + net.chips[r], :, cols].astype(f32)
+
     step = 16
     for t in (1, 3, 2, 0):
         s = net.z(t)
         net.wait(apl(t), am_pair + t)
-        base, cols = 4 * (t // 3), slice(768 * (t % 3), 768 * (t % 3) + 768)
-        for r in (1, 2, 3, 0):
-            total = amp[s, net.core, net.chips[r]].astype(f32)
-            total = total + esg[base + net.chips[r], :, cols].astype(f32)
-            if r == 0:
-                aso[s] = total
-            else:
-                amp[s, net.core, net.chips[r]] = total.astype(bf16)
-                net.send(
-                    amp.at[s, net.core, net.chips[r]],
-                    axl.at[s, r - 1],
-                    am_chip + 4 * t + r,
-                    (net.peer(r), m),
-                )
+        for r in (1, 2, 3):
+            part = amp.at[s, net.core, net.chips[r]]
+            part[...] = am_total(t, r).astype(bf16)
+            net.send(part, axl.at[s, r - 1], am_chip + 4 * t + r, (net.peer(r), m))
         for _ in range(4):
             pairwise = pair_chunk(step, pairwise)
             step += 1
@@ -984,7 +1019,7 @@
 
     def am_arrive(t):
         s = net.z(t)
-        total = aso[s]
+        total = am_total(t, 0)
         for r in (1, 2, 3):
             net.wait(axl.at[s, r - 1], am_chip + 4 * t + r)
             total = total + axl[s, r - 1].astype(f32)
@@ -992,7 +1027,7 @@
             azs[s] = total.astype(bf16)
             am_z.send(t, azs.at[s])
         else:
-            aso[s] = total
+            aso[...] = total
 
     am_arrive(1)
 
@@ -1012,7 +1047,7 @@
     am_arrive(3)
     am_arrive(2)
 
-    total = eso[...]
+    total = esp[net.core, net.chip].astype(f32) + epl[net.chip].astype(f32)
     for r in (1, 2, 3):
         net.wait(exl.at[r - 1], es_chip + r)
         total = total + exl[r - 1].astype(f32)
@@ -1056,7 +1091,7 @@
 
     unpack_out(o_line, opl, ops, out_o)
     unpack_out(r_line, rpl, rps, res_o)
-    total = aso[m]
+    total = aso[...]
     for t in (1, 3, 2):
         total = total + azl[am_z.wait(t)].astype(f32)
     at_o[0] = total[:, 384:576]
@@ -1079,7 +1114,7 @@
         V((8, 32, 1280), bf16), V((4, 8, 96, 768), bf16), V((8, 96, 2304), bf16),
         V((4, 768, 128), bf16), V((4, 768, 128), bf16),
         V((8, 1152), f32), V((4, 8, 1152), f32), V((6, 8, 768), f32), V((8, 8, 384), f32),
-        V((2, PAIRS, 256, 256), bf16), V((2, 1024, 256), bf16),
+        V((2, PAIRS, 256, 256), bf16),
         V((512, 768), f32), V((512, 128), f32), V((512, 768), bf16),
         V((512, 768), bf16), V((512, 768), bf16), V((128, 768), bf16), V((2, 1024, 256), f32),
         V((128, 768), bf16), V((128, 768), f32), V((128, 768), f32), V((128, 768), f32),
@@ -1088,17 +1123,17 @@
         V((4, 128, 1536), bf16), V((4, 128, 768), bf16), V((4, 128, 768), bf16),
         V((4, 128, 768), bf16), V((4, 128, 768), bf16), V((128, 768), f32), V((128, 768), f32),
         V((2, 4, 96, 2304), bf16), V((4, 96, 2304), bf16), V((3, 96, 2304), bf16),
-        V((96, 2304), f32),
         V((4, 512, 384), bf16), V((512, 768), f32), V((512, 768), f32), V((128, 768), bf16),
         V((128, 768), bf16), V((256, 768), bf16), V((4, 256, 384), bf16),
         V((4, 128, 768), bf16), V((4, 128, 768), bf16),
         V((4, 2, 4, 96, 768), bf16), V((4, 3, 96, 768), bf16),
-        V((4, 96, 768), f32), V((4, 96, 768), bf16), V((4, 96, 768), bf16),
+        V((96, 768), f32), V((4, 96, 768), bf16), V((4, 96, 768), bf16),
         V((4, 8, 1152), f32), V((4, 8, 1152), f32), V((8, 8, 1152), f32),
         V((2, 4, 32, 128), f32), V((4, 32, 128), f32), V((4, 32, 128), f32), V((4, 32, 128), f32),
         V((32, 256), f32), V((4, 32, 256), f32),
         V((4, 192, 128), bf16), V((4, 192, 128), bf16), V((4, 192, 128), bf16),
         V((4, 192, 128), bf16), V((256, 64), f32), V((256, 128), f32),
+        V((8, 256), f32),
         pltpu.SemaphoreType.DMA((160,)), pltpu.SemaphoreType.DMA((160,)),
         pltpu.SemaphoreType.DMA((2,)),
     ]
@@ -1111,7 +1146,9 @@
     return pl.pallas_call(
         layer_kernel,
         out_shape=tuple(jax.ShapeDtypeStruct(s, t) for s, t in outs),
-        in_specs=[pl.BlockSpec(memory_space=pl.ANY) if i == 5 else whole for i in range(9)],
+        in_specs=[whole] * 9
+        + [pl.BlockSpec(memory_space=pl.ANY), whole]
+        + [pl.BlockSpec(memory_space=pltpu.SMEM)] * 3,
         out_specs=(whole,) * len(outs),
         scratch_shapes=scratch,
         compiler_params=pltpu.CompilerParams(
@@ -1230,46 +1267,7 @@
     shrink_weight, shrink_state, modulate_weight, modulate_state, pair_weight, pair_state,
     class_weight, class_state,
 ):
-    m = lax.axis_index("mp")
     classes = class_weight.shape[0]
-    am = jnp.concatenate(
-        [attend_weight[:, 1], attend_weight[:, 2], attend_weight[:, 0], merge_weight.T], axis=1
-    ).astype(bf16)
-    es = jnp.concatenate(
-        [expand_weight[:, 0], expand_weight[:, 1], shrink_weight.T], axis=1
-    ).astype(bf16)
-    ms = jnp.concatenate(
-        [
-            jnp.pad(class_weight.T, ((0, 0), (0, 64 - classes))),
-            jnp.pad(pair_weight, ((0, 0), (0, 52))),
-            modulate_weight.reshape(32, 1152),
-        ],
-        axis=1,
-    ).astype(bf16)
-
-    def packed(v):
-        low = v[:, 128:]
-        return jnp.concatenate([v[:, :128], jnp.concatenate([low[:256], low[256:]], axis=1)], axis=0)
-
-    table = jnp.asarray(PATTERNS)
-    layout = (bucket_layout[:, None] == jnp.arange(5, dtype=jnp.int32)).astype(jnp.int32)
-    unit_slot = jnp.sum(layout[:, :, None] * table[None], axis=1)
-    pick_slot = (unit_slot[..., None] == jnp.arange(4, dtype=jnp.int32)).astype(jnp.int32)
-    unit_bin = jnp.sum(pick_slot * time_bins[:, None, :], axis=-1).reshape(8)
-    unit_class = jnp.sum(pick_slot * fold_class[:, None, :], axis=-1).reshape(8)
-    sinus = time_features(unit_bin, 256)
-    pick = (unit_class[:, None] == jnp.arange(128, dtype=jnp.int32)).astype(bf16)
-    mine = jnp.sum(
-        unit_slot * (jnp.arange(4, dtype=jnp.int32)[None] == m).astype(jnp.int32),
-        axis=1,
-        keepdims=True,
-    )
-    seen = jnp.where(unit_slot == mine, 0.0, MASKED)
-    mask = jnp.broadcast_to(seen[:, :, None], (2, 4, UNIT)).reshape(2, 256)
-
-    out, res, ds, pw, *grads = layer_call(
-        classes, ms, am, es, packed(residues), packed(out_grad), pair_input, sinus, pick, mask
-    )
 
     def thirds(v):
         return jnp.swapaxes(v, -3, -2).reshape(*v.shape[:-3], -1, v.shape[-1])
@@ -1289,9 +1287,14 @@
         attend_state, merge_state, expand_state, shrink_state, modulate_state, pair_state,
         class_state,
     )
+    flat = [view(master) for view, master in zip(views, masters)]
+    out, res, ds, pw, *grads = layer_call(
+        classes, flat[0].reshape(3, 96, 192), *flat[1:4], flat[4].reshape(6, 32, 192), *flat[5:],
+        residues.T, out_grad.T, pair_input, time_features(jnp.arange(128), 256), bucket_layout,
+        time_bins, fold_class,
+    )
     groups = []
-    for view, master, state, grad in zip(views, masters, states, grads):
-        master = view(master)
+    for view, master, state, grad in zip(views, flat, states, grads):
         groups += [master, view(state), grad.reshape(master.shape)]
     out, res, pair_grad, *results = finish_call(ds, pw, out, res, *groups)
 

time: 193 us -> 180 us (0.933)
  other arithmetic: 8.93 us -> 0.98 us
  local copies, waits for them, and re-layouts: 5.32 us -> 0 us
    concatenate x3 -> x0, other arithmetic: 2.42 us -> none  [the longest x1 0.86 us: packed(): jnp.concatenate([v[:, :128], jnp.concatenate([low[:256], low[256:]], axis...]
    another operation x5 -> x0, other arithmetic: 2.4 us -> none
where the time goes in v4:
time: 180 us
  Pallas kernels  178 us (99%)
    pallas_call x1, Pallas kernels, layer_call(): pl.pallas_call(layer_kernel, out_shape=tuple((jax.ShapeDtypeStruct(s, t)...  164 us
    pallas_call x1, Pallas kernels, finish_call(): pl.pallas_call(finish_kernel, grid=(4,), out_shape=tuple(outs), in_specs=...  14.2 us

profile of v4, /device:TPU:0, one launch (start us, length us, event | category | flops | bytes accessed | tf_op | source)
XLA Modules:
  0.0 179.8 jit_solution(1929688689289658482)
XLA Ops:
  0.7 0.3 multiply_sine_fusion
  1.0 0.7 pad_maximum_fusion.waves
  1.6 163.7 %layer.1 = (bf16[512,192]{1,0:T(8,128)(2,1)}, bf16[512,192]{1,0:T(8,128)(2,1)}, bf16[2,1024,256]{2,1,0:T(8,128)(2,1)}, bf16[16,256]{1,0:T(8,128)(2,1)}, f32[3,96...) custom-call(f32[3,96,192]{2,1,0:T(8,128)} %bitcast.42, ...), custom_call_target="tpu_custom_call" | custom-call | tf_op jit(solution)/shard_map/layer/pallas_call | solution.py:1146
  165.4 14.2 %finish.1 = (bf16[192,512]{1,0:T(8,128)(2,1)}, bf16[192,512]{1,0:T(8,128)(2,1)}, bf16[2,64,256,256]{3,2,1,0:T(8,128)(2,1)}, f32[2,288,192]{2,1,0:T(8,128)}, f32[...) custom-call(bf16[2,1024,256]{2,1,0:T(8,128)(2,1)} %get-tuple-element, ...), custom_call_target="tpu_custom_call" | custom-call | tf_op jit(solution)/shard_map/finish/pallas_call | solution.py:1252
  (1 shorter events, 0.0 us)

commit v5 on v4

--- a/solution.py
+++ b/solution.py
@@ -894,18 +894,6 @@
                 low = block[s, 128:192, :].astype(f32)[:, 64 * w : 64 * w + 64]
                 to[rows, :] = jnp.concatenate([high, low], axis=-1).astype(bf16)
 
-    for t in (1, 3, 2):
-        f_line.wait(t)
-    done = []
-    for w in range(2):
-        half = slice(w * UNIT, w * UNIT + UNIT)
-        fed = fpo[half, :]
-        for t in (1, 3, 2):
-            fed = fed + fl[net.z(t), half, :].astype(f32)
-        own_sums[w][5] = unit_sum(unpack(gg, w, m) * fed)
-        done.append(mid[half, :] + mod_row(5, w) * fed)
-    pack(o_line, jnp.concatenate(done, axis=0), ops)
-
     for s in range(4):
         cols = slice(192 * s, 192 * s + 192)
         dkv[s] = jnp.concatenate([dkf[:, cols], dvf[:, cols]], axis=-1).astype(bf16)
@@ -916,7 +904,14 @@
     def apl(t):
         return esg.at[pl.ds(4 * (t // 3), 4), :, 768 * (t % 3) : 768 * (t % 3) + 768]
 
-    for t in (1, 3, 2, 0):
+    am_chip = net.sems(16)
+
+    def am_total(t, r):
+        base, cols = 4 * (t // 3), slice(768 * (t % 3), 768 * (t % 3) + 768)
+        total = amp[net.z(t), net.core, net.chips[r]].astype(f32)
+        return total + esg[base + net.chips[r], :, cols].astype(f32)
+
+    def am_grads(t):
         s = net.z(t)
         for h in range(2):
             cols = slice(384 * h, 384 * h + 384)
@@ -926,6 +921,33 @@
                     part = value[96 * i : 96 * i + 96, :].astype(bf16)
                     amp[s, i % 2, 2 * h + i // 2, :, at : at + 384] = part
         net.send(amp.at[s, 1 - net.core], apl(t), am_pair + t, (net.partner, m))
+
+    def am_out(t):
+        s = net.z(t)
+        net.wait(apl(t), am_pair + t)
+        for r in (1, 2, 3):
+            part = amp.at[s, net.core, net.chips[r]]
+            part[...] = am_total(t, r).astype(bf16)
+            net.send(part, axl.at[s, r - 1], am_chip + 4 * t + r, (net.peer(r), m))
+
+    am_grads(1)
+    am_grads(3)
+    am_out(1)
+    am_grads(2)
+    am_out(3)
+    am_grads(0)
+    am_out(2)
+
+    for t in (1, 3, 2):
+        f_line.wait(t)
+    fed_done = []
+    for w in range(2):
+        half = slice(w * UNIT, w * UNIT + UNIT)
+        fed = fpo[half, :]
+        for t in (1, 3, 2):
+            fed = fed + fl[net.z(t), half, :].astype(f32)
+        own_sums[w][5] = unit_sum(unpack(gg, w, m) * fed)
+        fed_done.append(mid[half, :] + mod_row(5, w) * fed)
 
     for w in range(2):
         rows = slice(w * 256, w * 256 + 256)
@@ -938,13 +960,6 @@
         total = total + mm(rhs2[s, 0:128, :], weight(s, 384, 768), NT)
     for w in range(2):
         dkf[own(w), :] += total[w * UNIT : w * UNIT + UNIT, :]
-    p1_line = Zline(net, lambda s: p1l.at[s])
-    for t in (1, 3, 2):
-        s = net.z(t)
-        for w in range(2):
-            rows = pl.ds(pl.multiple_of(w * 256 + s * UNIT, UNIT), UNIT)
-            p1[s, w * UNIT : w * UNIT + UNIT, :] = dkf[rows, :].astype(bf16)
-        p1_line.send(t, p1.at[s])
 
     sums = [[], []]
     for u in range(8):
@@ -962,6 +977,14 @@
         mps[s] = jnp.concatenate([v[:, 192 * s : 192 * s + 192] for v in table], axis=-1)
     for t in (1, 3, 2):
         mod_sum.send(t, mps.at[net.z(t)])
+    p1_line = Zline(net, lambda s: p1l.at[s])
+    for t in (1, 3, 2):
+        s = net.z(t)
+        for w in range(2):
+            rows = pl.ds(pl.multiple_of(w * 256 + s * UNIT, UNIT), UNIT)
+            p1[s, w * UNIT : w * UNIT + UNIT, :] = dkf[rows, :].astype(bf16)
+        p1_line.send(t, p1.at[s])
+    pack(o_line, jnp.concatenate(fed_done, axis=0), ops)
 
     def pair_chunk(step, acc):
         slot = step % slots
@@ -977,24 +1000,8 @@
         return acc
 
     pairwise = jnp.zeros((GROUP, 256), f32)
-    am_chip = net.sems(16)
-
-    def am_total(t, r):
-        base, cols = 4 * (t // 3), slice(768 * (t % 3), 768 * (t % 3) + 768)
-        total = amp[net.z(t), net.core, net.chips[r]].astype(f32)
-        return total + esg[base + net.chips[r], :, cols].astype(f32)
-
-    step = 16
-    for t in (1, 3, 2, 0):
-        s = net.z(t)
-        net.wait(apl(t), am_pair + t)
-        for r in (1, 2, 3):
-            part = amp.at[s, net.core, net.chips[r]]
-            part[...] = am_total(t, r).astype(bf16)
-            net.send(part, axl.at[s, r - 1], am_chip + 4 * t + r, (net.peer(r), m))
-        for _ in range(4):
-            pairwise = pair_chunk(step, pairwise)
-            step += 1
+    for step in range(16, 32):
+        pairwise = pair_chunk(step, pairwise)
 
     for r in (1, 2, 3):
         bp_all.forward(r)
@@ -1029,7 +1036,26 @@
         else:
             aso[...] = total
 
+    net.wait(pwl, pw_pair)
+    pw_chip = net.sems(4)
+    for r in (1, 2, 3):
+        pwx[r] = pws[net.core, net.chips[r]] + pwl[net.chips[r]]
+        net.send(pwx.at[r], pwy.at[r], pw_chip + r, (net.peer(r), m))
+    pair_sum = pws[net.core, net.chip] + pwl[net.chip]
+
+    am_out(0)
     am_arrive(1)
+    am_arrive(3)
+
+    total = esp[net.core, net.chip].astype(f32) + epl[net.chip].astype(f32)
+    for r in (1, 2, 3):
+        net.wait(exl.at[r - 1], es_chip + r)
+        total = total + exl[r - 1].astype(f32)
+    for k in range(2):
+        ex_o[:, k, :] = total[:, 768 * k : 768 * k + 768]
+    sh_o[...] = total[:, 1536:2304]
+
+    am_arrive(2)
 
     for t in (1, 3, 2):
         p1_line.wait(t)
@@ -1043,24 +1069,6 @@
         back = norm_back(upstream, n1[own(w), :], sp1[own(w), :][:, 0:1], mod_row(1, w))
         done.append(p2o[half, :] + back)
     pack(r_line, jnp.concatenate(done, axis=0), rps)
-
-    am_arrive(3)
-    am_arrive(2)
-
-    total = esp[net.core, net.chip].astype(f32) + epl[net.chip].astype(f32)
-    for r in (1, 2, 3):
-        net.wait(exl.at[r - 1], es_chip + r)
-        total = total + exl[r - 1].astype(f32)
-    for k in range(2):
-        ex_o[:, k, :] = total[:, 768 * k : 768 * k + 768]
-    sh_o[...] = total[:, 1536:2304]
-
-    net.wait(pwl, pw_pair)
-    pw_chip = net.sems(4)
-    for r in (1, 2, 3):
-        pwx[r] = pws[net.core, net.chips[r]] + pwl[net.chips[r]]
-        net.send(pwx.at[r], pwy.at[r], pw_chip + r, (net.peer(r), m))
-    pair_sum = pws[net.core, net.chip] + pwl[net.chip]
 
     for r in (1, 2, 3):
         mr_all.forward(r)

time: 180 us -> 178 us (0.989)
  Pallas kernels: 178 us -> 176 us
    pallas_call x1, Pallas kernels: 164 us -> 162 us  [layer_call(): pl.pallas_call(layer_kernel, out_shape=tuple((jax.ShapeDtypeStruct(s, t)...]
where the time goes in v5:
time: 178 us
  Pallas kernels  176 us (99%)
    pallas_call x1, Pallas kernels, layer_call(): pl.pallas_call(layer_kernel, out_shape=tuple((jax.ShapeDtypeStruct(s, t)...  162 us
    pallas_call x1, Pallas kernels, finish_call(): pl.pallas_call(finish_kernel, grid=(4,), out_shape=tuple(outs), in_specs=...  14.2 us

profile of v5, /device:TPU:0, one launch (start us, length us, event | category | flops | bytes accessed | tf_op | source)
XLA Modules:
  0.0 177.9 jit_solution(4159015524731185851)
XLA Ops:
  0.7 0.3 multiply_sine_fusion
  1.0 0.7 pad_maximum_fusion.waves
  1.6 161.8 %layer.1 = (bf16[512,192]{1,0:T(8,128)(2,1)}, bf16[512,192]{1,0:T(8,128)(2,1)}, bf16[2,1024,256]{2,1,0:T(8,128)(2,1)}, bf16[16,256]{1,0:T(8,128)(2,1)}, f32[3,96...) custom-call(f32[3,96,192]{2,1,0:T(8,128)} %bitcast.42, ...), custom_call_target="tpu_custom_call" | custom-call | tf_op jit(solution)/shard_map/layer/pallas_call | solution.py:1154
  163.5 14.2 %finish.1 = (bf16[192,512]{1,0:T(8,128)(2,1)}, bf16[192,512]{1,0:T(8,128)(2,1)}, bf16[2,64,256,256]{3,2,1,0:T(8,128)(2,1)}, f32[2,288,192]{2,1,0:T(8,128)}, f32[...) custom-call(bf16[2,1024,256]{2,1,0:T(8,128)(2,1)} %get-tuple-element, ...), custom_call_target="tpu_custom_call" | custom-call | tf_op jit(solution)/shard_map/finish/pallas_call | solution.py:1260
  (1 shorter events, 0.0 us)

commit v6 on v5

--- a/solution.py
+++ b/solution.py
@@ -340,6 +340,10 @@
     )
 
 
+ANGLES = (1000.0 * (np.arange(128, dtype=np.float32)[:, None] + 0.5) / TBINS) * np.exp(
+    -math.log(10000.0) * np.arange(128, dtype=np.float32) / 128
+)
+WAVES = np.concatenate([np.sin(ANGLES), np.cos(ANGLES)], axis=-1).astype(np.float32)
 RATES = (
     2.0 / math.sqrt(D),
     2.0 / math.sqrt(D // 8),
@@ -1072,7 +1076,6 @@
 
     for r in (1, 2, 3):
         mr_all.forward(r)
-    am_arrive(0)
 
     mr_all.finish()
     before = bpg[:, :, 0:256].reshape(64, 256)
@@ -1099,6 +1102,7 @@
 
     unpack_out(o_line, opl, ops, out_o)
     unpack_out(r_line, rpl, rps, res_o)
+    am_arrive(0)
     total = aso[...]
     for t in (1, 3, 2):
         total = total + azl[am_z.wait(t)].astype(f32)
@@ -1298,7 +1302,7 @@
     flat = [view(master) for view, master in zip(views, masters)]
     out, res, ds, pw, *grads = layer_call(
         classes, flat[0].reshape(3, 96, 192), *flat[1:4], flat[4].reshape(6, 32, 192), *flat[5:],
-        residues.T, out_grad.T, pair_input, time_features(jnp.arange(128), 256), bucket_layout,
+        residues.T, out_grad.T, pair_input, jnp.asarray(WAVES), bucket_layout,
         time_bins, fold_class,
     )
     groups = []

time: 178 us -> 177 us (level)
  no operation moved by 1% of the time
where the time goes in v6:
time: 177 us; the launch traced here: 176 us
  Pallas kernels  175 us (99%)
    pallas_call x1, Pallas kernels, layer_call(): pl.pallas_call(layer_kernel, out_shape=tuple((jax.ShapeDtypeStruct(s, t)...  161 us
    pallas_call x1, Pallas kernels, finish_call(): pl.pallas_call(finish_kernel, grid=(4,), out_shape=tuple(outs), in_specs=...  14.2 us

profile of v6, /device:TPU:0, one launch (start us, length us, event | category | flops | bytes accessed | tf_op | source)
XLA Modules:
  0.0 176.0 jit_solution(18155467444087602318)
XLA Ops:
  0.7 160.9 %layer.1 = (bf16[512,192]{1,0:T(8,128)(2,1)}, bf16[512,192]{1,0:T(8,128)(2,1)}, bf16[2,1024,256]{2,1,0:T(8,128)(2,1)}, bf16[16,256]{1,0:T(8,128)(2,1)}, f32[3,96...) custom-call(f32[3,96,192]{2,1,0:T(8,128)} %bitcast.42, ...), custom_call_target="tpu_custom_call" | custom-call | tf_op jit(solution)/shard_map/layer/pallas_call | solution.py:1158
  161.6 14.2 %finish.1 = (bf16[192,512]{1,0:T(8,128)(2,1)}, bf16[192,512]{1,0:T(8,128)(2,1)}, bf16[2,64,256,256]{3,2,1,0:T(8,128)(2,1)}, f32[2,288,192]{2,1,0:T(8,128)}, f32[...) custom-call(bf16[2,1024,256]{2,1,0:T(8,128)(2,1)} %get-tuple-element, ...), custom_call_target="tpu_custom_call" | custom-call | tf_op jit(solution)/shard_map/finish/pallas_call | solution.py:1264
